TPU v7x, 256 devices: a whole 4x4x8 slice. The times are simulated.
256 devices in a mesh: seq: 64 (over z, x, y_hi), tp: 4 (over y_lo, core).
Axes of the slice: x: 4, y: 4 (y_hi: 2, y_lo: 2; y = y_hi * 2 + y_lo), z: 8, core: 2. Of those that a mesh axis runs over, the one named last changes fastest.
Arguments:
- tokens: bfloat16 [36864, 3072], P('seq', 'tp'), may hold values from -6 to 6, as said below
- norm_gain: float32 [3072], replicated, may hold values from 0.1 to 1.9
- w_qkv: bfloat16 [3072, 3, 1536], P(None, None, 'tp'), may hold values from -0.649519 to 0.649519, as said below
- w_out: bfloat16 [1536, 3072], P('tp'), may hold values from -2.5 to 2.5
- sink_logit: float32 [16], P('tp'), may hold values from 4 to 8
- segment_ids: int32 [36864], P('seq'), may hold values from 0 to 30, as said below
- positions: int32 [36864], P('seq'), may hold values from 0 to 32831, as said below
- padding_mask: int32 [36864], P('seq'), may hold values from 0 to 1, as said below
Outputs:
- attn_out: bfloat16 [36864, 3072], P('seq', 'tp')
- kv_cache: bfloat16 [2, 36864, 1536], P(None, 'seq', 'tp')
Inputs may be any that keep to these rules, and one draw needn't show every extreme that they name: `segment_ids`: segment 0 is one long prompt covering tokens 0 to 32831; after it come short prompts with ids rising by one: first one shorter prompt if the short region is not filled otherwise, then consecutive pairs whose two lengths sum to 256, then a last prompt of exactly 256 tokens ending at the stream's end. `positions`: the index of each token within its prompt, counted from 0 at the prompt's first token. `padding_mask`: zero only on trailing tokens of short prompts: each short prompt has at most half of its tokens padded at its end, the last prompt 1 to 128; the long prompt has none. `w_qkv`: entries within the stated bound. `tokens`: entries within the stated bound.
All inputs are finite; a program needn't handle non-finite values.
Results may differ from a plain program's by a relative error of at most 0.015.
Values may be sent and summed in bfloat16 or wider, within the bound.
A program may use at most 128 MiB of HBM per device.

v0:
```python
import jax
import jax.numpy as jnp
from jax import lax
from jax.sharding import PartitionSpec as P

WINDOW = 4096
SINKS = 4


EPS = 1e-05
THETA = 10000.0


def from_root(value, axis, source):
    kept = jnp.where(lax.axis_index(axis) == source, value, 0).astype(value.dtype)
    return lax.psum(kept, axis)


def from_behind(value, axis, by):
    count = lax.axis_size(axis)
    pairs = [(i, i + by) for i in range(count) if 0 <= i + by < count]
    return lax.ppermute(value, axis, pairs)


def rotate(values, pos):
    half = values.shape[-1] // 2
    freq = THETA ** (-(jnp.arange(half, dtype=jnp.float32) * 2.0 / values.shape[-1]))
    angle = pos.astype(jnp.float32)[:, None] * freq[None, :]
    cosine = jnp.cos(angle)[:, None, :]
    sine = jnp.sin(angle)[:, None, :]
    first = values[..., :half]
    second = values[..., half:]
    return jnp.concatenate(
        [first * cosine - second * sine, second * cosine + first * sine], axis=-1
    )


def shards(tokens, norm_gain, w_qkv, w_out, sink_logit, segment_ids, positions, padding_mask):
    rows = tokens.shape[0]
    whole = lax.all_gather(tokens, "tp", axis=1, tiled=True)
    xf = whole.astype(jnp.float32)
    meansq = jnp.mean(xf * xf, axis=-1, keepdims=True)
    normed = (xf * lax.rsqrt(meansq + EPS) * norm_gain).astype(jnp.bfloat16)
    heads_local = sink_logit.shape[0]
    width = w_qkv.shape[2]
    depth = width // heads_local
    model = w_qkv.shape[0]
    qkv = jnp.dot(normed, w_qkv.reshape(model, 3 * width), preferred_element_type=jnp.float32)
    qkv = qkv.reshape(rows, 3, heads_local, depth)
    query = rotate(qkv[:, 0], positions).astype(jnp.bfloat16)
    key = rotate(qkv[:, 1], positions).astype(jnp.bfloat16)
    value = qkv[:, 2].astype(jnp.bfloat16)
    keep = padding_mask[:, None, None].astype(jnp.bfloat16)
    kv_cache = jnp.stack([(key * keep).reshape(rows, width), (value * keep).reshape(rows, width)])
    marks = jnp.stack([segment_ids, positions, padding_mask])
    here = lax.axis_index("seq")
    qrows = here * rows + jnp.arange(rows, dtype=jnp.int32)
    scale = depth ** (-0.5)

    def attend(state, block, block_marks, start, leading):
        top, total, acc = state
        count = block.shape[1]
        kblk = block[0].reshape(count, heads_local, depth)
        vblk = block[1].reshape(count, heads_local, depth)
        bias = jnp.where(block_marks[1][None, None, :] < SINKS, sink_logit[:, None, None], 0.0)
        scores = (
            jnp.einsum("qhd,khd->hqk", query, kblk, preferred_element_type=jnp.float32) * scale
            + bias
        )
        krows = start + jnp.arange(count, dtype=jnp.int32)
        same = block_marks[0][None, :] == segment_ids[:, None]
        usable = (block_marks[2][None, :] == 1) | (krows[None, :] == qrows[:, None])
        if leading:
            seen = (krows[None, :] <= qrows[:, None]) & same & usable
        else:
            seen = (
                (krows[None, :] >= SINKS)
                & (krows[None, :] <= qrows[:, None])
                & (qrows[:, None] - krows[None, :] < WINDOW)
            )
            seen = seen & same & usable
        newtop = jnp.maximum(top, jnp.max(jnp.where(seen[None], scores, -1e30), axis=-1))
        fade = jnp.exp(top - newtop)
        weights = jnp.where(seen[None], jnp.exp(scores - newtop[..., None]), 0.0)
        total = total * fade + jnp.sum(weights, axis=-1)
        acc = acc * fade[..., None] + jnp.einsum(
            "hqk,khd->hqd", weights.astype(jnp.bfloat16), vblk, preferred_element_type=jnp.float32
        )
        return (newtop, total, acc)

    state = (
        jnp.full((heads_local, rows), -1e30, jnp.float32),
        jnp.zeros((heads_local, rows), jnp.float32),
        jnp.zeros((heads_local, rows, depth), jnp.float32),
    )
    own = jnp.stack([key.reshape(rows, width), value.reshape(rows, width)])
    state = attend(state, own, marks, here * rows, False)
    first_rows = own[:, :SINKS]
    sink_block, sink_marks = (
        from_root(first_rows, "seq", 0),
        from_root(marks[:, :SINKS], "seq", 0),
    )
    state = attend(state, sink_block, sink_marks, 0, True)
    reach = (WINDOW - 1 + rows - 1) // rows

    def step(turn, carry):
        inner, block, block_marks = carry
        block, block_marks = from_behind((block, block_marks), "seq", 1)
        inner = attend(inner, block, block_marks, (here - turn) * rows, False)
        return (inner, block, block_marks)

    state, _, _ = lax.fori_loop(1, reach + 1, step, (state, kv_cache, marks))
    top, total, acc = state
    mixed = (acc / total[..., None]).astype(jnp.bfloat16)
    mixed = mixed.transpose(1, 0, 2).reshape(rows, width)
    partial_value = jnp.dot(mixed, w_out, preferred_element_type=jnp.float32)
    summed = lax.psum_scatter(
        partial_value.astype(jnp.bfloat16), "tp", scatter_dimension=1, tiled=True
    )
    return (summed, kv_cache)


def solution(mesh):
    return jax.shard_map(
        shards,
        mesh=mesh,
        in_specs=(
            P("seq", "tp"),
            P(),
            P(None, None, "tp"),
            P("tp", None),
            P("tp"),
            P("seq"),
            P("seq"),
            P("seq"),
        ),
        out_specs=(P("seq", "tp"), P(None, "seq", "tp")),
        check_vma=False,
    )
```

profile of v0, /device:TPU:241, one launch (start us, length us, event | category | flops | bytes accessed | tf_op | source)
XLA Modules:
  0.0 654.1 jit_solution(10537814505922396946)
XLA Ops:
  10.6 15.0 %psum.14 = s32[3,4]{1,0:T(4,128)S(1)} all-reduce(s32[3,4]{1,0:T(4,128)S(1)} %slice_select_fusion), channel_id=1, replica_groups=mesh['seq'=64,'tp'=4] {'seq'}, use_global_device_ids=true, to_apply=%region_2.3 | all-reduce | flops 12 | bytes 96 | tf_op jit(solution)/shard_map/psum | solution.py:16
  27.6 10.4 %copy.28 = bf16[3072,3,384]{0,2,1:T(8,128)(2,1)} copy(bf16[3072,3,384]{2,0,1:T(8,128)(2,1)} %param.12) | data formatting | bytes 14155776 | tf_op args[2]
  41.6 12.2 %all-gather.2.cloned.1.call-done = bf16[576,3072]{1,0:T(8,128)(2,1)} async-done(((bf16[576,768]{1,0:T(8,128)(2,1)}), bf16[576,3072]{1,0:T(8,128)(2,1)}) %all-gather.2.cloned.1.call-update) | async-done | bytes 3538960 | tf_op jit(solution)/shard_map/all_gather | solution.py:40
  56.6 9.2 %fusion.21 = f32[576,3,4,96]{0,3,2,1:T(8,128)S(1)} fusion(bf16[3,4,96,3072]{3,2,1,0:T(8,128)(2,1)} %bitcast.48, bf16[576,3072]{1,0:T(8,128)(2,1)} %all-gather.2.cloned.1.call-done, f32[3072]{0:T(1024)S(1)} %copy-done.24, f32[576]{0:T(1024)S(1)} %add_rsqrt_fusion), kind=kOutput, calls=%fused_computation.36 | convolution fusion | flops 4083941376 | bytes 13285632 | tf_op jit(solution)/shard_map/dot_general | solution.py:48
  70.3 140.6 %psum.15 = bf16[2,4,384]{2,1,0:T(4,128)(2,1)S(1)} all-reduce(bf16[2,4,384]{2,1,0:T(4,128)(2,1)S(1)} %fusion.48), channel_id=1, replica_groups=mesh['seq'=64,'tp'=4] {'seq'}, use_global_device_ids=true, to_apply=%region_3.4 | all-reduce | flops 3072 | bytes 12288 | tf_op jit(solution)/shard_map/psum | solution.py:16
  227.7 324.7 %while.22 = (s32[]{:T(128)}, f32[4,576]{1,0:T(4,128)S(1)}, f32[4,576]{1,0:T(4,128)S(1)}, f32[4,576,96]{1,2,0:T(8,128)}, bf16[2,576,384]{2,1,0:T(8,128)(2,1)}, /*...) while((s32[]{:T(128)}, f32[4,576]{1,0:T(4,128)S(1)}, ...), condition=%wide.region_10.11_spmd.clone, body=%wide.region_7.10_spmd.clone.sunk | while | flops 531957888 | bytes 39623408 | solution.py:112
  227.7 6.0 collective-permute-start
  233.7 5.0 collective-permute-start.1
  240.6 8.7 %collective-permute-done.1 = bf16[2,576,384]{2,1,0:T(8,128)(2,1)S(1)} collective-permute-done((bf16[2,576,384]{2,1,0:T(8,128)(2,1)}, bf16[2,576,384]{2,1,0:T(8,128)(2,1)S(1)}, u32[]{:S(2)}, u32[]{:S(2)}) %collective-permute-start.1) | collective-permute-done | bytes 884768 | tf_op jit(solution)/shard_map/while/body/eval_jaxpr/ppermute | solution.py:22
  262.6 5.9 collective-permute-start
  268.4 5.1 collective-permute-start.1
  275.4 11.6 %collective-permute-done.1 = bf16[2,576,384]{2,1,0:T(8,128)(2,1)S(1)} collective-permute-done((bf16[2,576,384]{2,1,0:T(8,128)(2,1)}, bf16[2,576,384]{2,1,0:T(8,128)(2,1)S(1)}, u32[]{:S(2)}, u32[]{:S(2)}) %collective-permute-start.1) | collective-permute-done | bytes 884768 | tf_op jit(solution)/shard_map/while/body/eval_jaxpr/ppermute | solution.py:22
  300.3 5.8 collective-permute-start
  306.1 5.2 collective-permute-start.1
  313.2 12.9 %collective-permute-done.1 = bf16[2,576,384]{2,1,0:T(8,128)(2,1)S(1)} collective-permute-done((bf16[2,576,384]{2,1,0:T(8,128)(2,1)}, bf16[2,576,384]{2,1,0:T(8,128)(2,1)S(1)}, u32[]{:S(2)}, u32[]{:S(2)}) %collective-permute-start.1) | collective-permute-done | bytes 884768 | tf_op jit(solution)/shard_map/while/body/eval_jaxpr/ppermute | solution.py:22
  339.5 6.1 collective-permute-start
  345.6 7.0 %collective-permute-start.1 = (bf16[2,576,384]{2,1,0:T(8,128)(2,1)}, bf16[2,576,384]{2,1,0:T(8,128)(2,1)S(1)}, u32[]{:S(2)}, u32[]{:S(2)}) collective-permute-start(bf16[2,576,384]{2,1,0:T(8,128)(2,1)} %get-tuple-element.389), channel_id=1, source_target_pairs={{0,4},{4,8},{8,12},{12,16},{16,20},{20,24},{24,28},{28,32},{32,36}... | collective-permute-start | bytes 2654216 | tf_op jit(solution)/shard_map/while/body/eval_jaxpr/ppermute | solution.py:22
  354.4 16.2 %collective-permute-done.1 = bf16[2,576,384]{2,1,0:T(8,128)(2,1)S(1)} collective-permute-done((bf16[2,576,384]{2,1,0:T(8,128)(2,1)}, bf16[2,576,384]{2,1,0:T(8,128)(2,1)S(1)}, u32[]{:S(2)}, u32[]{:S(2)}) %collective-permute-start.1) | collective-permute-done | bytes 884768 | tf_op jit(solution)/shard_map/while/body/eval_jaxpr/ppermute | solution.py:22
  383.9 7.2 %collective-permute-start = (s32[3,576]{1,0:T(4,128)S(1)}, s32[3,576]{1,0:T(4,128)S(1)}, u32[]{:S(2)}, u32[]{:S(2)}) collective-permute-start(s32[3,576]{1,0:T(4,128)S(1)} %get-tuple-element.390), channel_id=1, source_target_pairs={{0,4},{4,8},{8,12},{12,16},{16,20},{20,24},{24,28},{28,32},{32,36}... | collective-permute-start | bytes 20744 | tf_op jit(solution)/shard_map/while/body/eval_jaxpr/ppermute | solution.py:22
  391.1 5.5 collective-permute-start.1
  398.5 17.7 %collective-permute-done.1 = bf16[2,576,384]{2,1,0:T(8,128)(2,1)S(1)} collective-permute-done((bf16[2,576,384]{2,1,0:T(8,128)(2,1)}, bf16[2,576,384]{2,1,0:T(8,128)(2,1)S(1)}, u32[]{:S(2)}, u32[]{:S(2)}) %collective-permute-start.1) | collective-permute-done | bytes 884768 | tf_op jit(solution)/shard_map/while/body/eval_jaxpr/ppermute | solution.py:22
  429.6 6.1 collective-permute-start
  435.7 4.9 collective-permute-start.1
  442.5 16.9 %collective-permute-done.1 = bf16[2,576,384]{2,1,0:T(8,128)(2,1)S(1)} collective-permute-done((bf16[2,576,384]{2,1,0:T(8,128)(2,1)}, bf16[2,576,384]{2,1,0:T(8,128)(2,1)S(1)}, u32[]{:S(2)}, u32[]{:S(2)}) %collective-permute-start.1) | collective-permute-done | bytes 884768 | tf_op jit(solution)/shard_map/while/body/eval_jaxpr/ppermute | solution.py:22
  464.4 3.3 select_reduce_fusion.4
  472.7 5.5 collective-permute-start
  482.5 17.9 %collective-permute-done.1 = bf16[2,576,384]{2,1,0:T(8,128)(2,1)S(1)} collective-permute-done((bf16[2,576,384]{2,1,0:T(8,128)(2,1)}, bf16[2,576,384]{2,1,0:T(8,128)(2,1)S(1)}, u32[]{:S(2)}, u32[]{:S(2)}) %collective-permute-start.1) | collective-permute-done | bytes 884768 | tf_op jit(solution)/shard_map/while/body/eval_jaxpr/ppermute | solution.py:22
  505.5 3.3 select_reduce_fusion.4
  513.7 3.9 collective-permute-start
  521.7 17.3 %collective-permute-done.1 = bf16[2,576,384]{2,1,0:T(8,128)(2,1)S(1)} collective-permute-done((bf16[2,576,384]{2,1,0:T(8,128)(2,1)}, bf16[2,576,384]{2,1,0:T(8,128)(2,1)S(1)}, u32[]{:S(2)}, u32[]{:S(2)}) %collective-permute-start.1) | collective-permute-done | bytes 884768 | tf_op jit(solution)/shard_map/while/body/eval_jaxpr/ppermute | solution.py:22
  553.7 3.8 convolution_convert_fusion
  557.5 89.7 %reduce-scatter.2.cloned.1.call-done = bf16[576,768]{1,0:T(8,128)(2,1)} async-done(((bf16[576,3072]{1,0:T(8,128)(2,1)}), bf16[576,768]{1,0:T(8,128)(2,1)}) %reduce-scatter.2.cloned.1.call-update) | async-done | bytes 884752 | tf_op jit(solution)/shard_map/reduce_scatter | solution.py:117
  (307 shorter events, 153.0 us)
Async XLA Ops:
  7.2 546.5 %copy-start = (bf16[384,3072]{1,0:T(8,128)(2,1)S(1)}, bf16[384,3072]{1,0:T(8,128)(2,1)}, u32[]{:S(2)}) copy-start(bf16[384,3072]{1,0:T(8,128)(2,1)} %param.13) | copy-start | bytes 7077892
  7.2 46.6 %all-gather.2.cloned.1.call-start = ((), (), s32[]{:S(2)}) async-start(), calls=%async_computation.1 | async-start | bytes 4423680 | tf_op jit(solution)/shard_map/all_gather | solution.py:40
  7.9 639.3 %reduce-scatter.2.cloned.1.call-start = ((), (), s32[]{:S(2)}) async-start(), calls=%async_computation.2 | async-start | bytes 4423680 | tf_op jit(solution)/shard_map/reduce_scatter | solution.py:117
  27.6 10.4 %copy-start.17 = (f32[4]{0:T(128)S(1)}, f32[4]{0:T(128)}, u32[]{:S(2)}) copy-start(f32[4]{0:T(128)} %param.14) | copy-start | bytes 52
  27.6 11.1 %copy-start.15 = (s32[576]{0:T(1024)S(1)}, s32[576]{0:T(1024)}, u32[]{:S(2)}) copy-start(s32[576]{0:T(1024)} %param.17) | copy-start | bytes 6916
  27.6 11.1 %copy-start.16 = (s32[576]{0:T(1024)S(1)}, s32[576]{0:T(1024)}, u32[]{:S(2)}) copy-start(s32[576]{0:T(1024)} %param.16) | copy-start | bytes 6916
  27.6 11.2 %copy-start.14 = (s32[576]{0:T(1024)S(1)}, s32[576]{0:T(1024)}, u32[]{:S(2)}) copy-start(s32[576]{0:T(1024)} %param.15) | copy-start | bytes 6916
  27.6 29.0 %copy-start.24 = (f32[3072]{0:T(1024)S(1)}, f32[3072]{0:T(1024)}, u32[]{:S(2)}) copy-start(f32[3072]{0:T(1024)} %param.11) | copy-start | bytes 36868
  227.7 11.1 %collective-permute-start = (s32[3,576]{1,0:T(4,128)S(1)}, s32[3,576]{1,0:T(4,128)S(1)}, u32[]{:S(2)}, u32[]{:S(2)}) collective-permute-start(s32[3,576]{1,0:T(4,128)S(1)} %get-tuple-element.390), channel_id=1, source_target_pairs={{0,4},{4,8},{8,12},{12,16},{16,20},{20,24},{24,28},{28,32},{32,36}... | collective-permute-start | bytes 20744 | tf_op jit(solution)/shard_map/while/body/eval_jaxpr/ppermute | solution.py:22
  233.7 15.5 %collective-permute-start.1 = (bf16[2,576,384]{2,1,0:T(8,128)(2,1)}, bf16[2,576,384]{2,1,0:T(8,128)(2,1)S(1)}, u32[]{:S(2)}, u32[]{:S(2)}) collective-permute-start(bf16[2,576,384]{2,1,0:T(8,128)(2,1)} %get-tuple-element.389), channel_id=1, source_target_pairs={{0,4},{4,8},{8,12},{12,16},{16,20},{20,24},{24,28},{28,32},{32,36}... | collective-permute-start | bytes 2654216 | tf_op jit(solution)/shard_map/while/body/eval_jaxpr/ppermute | solution.py:22
  254.3 5.1 copy-start.3
  262.6 11.1 %collective-permute-start = (s32[3,576]{1,0:T(4,128)S(1)}, s32[3,576]{1,0:T(4,128)S(1)}, u32[]{:S(2)}, u32[]{:S(2)}) collective-permute-start(s32[3,576]{1,0:T(4,128)S(1)} %get-tuple-element.390), channel_id=1, source_target_pairs={{0,4},{4,8},{8,12},{12,16},{16,20},{20,24},{24,28},{28,32},{32,36}... | collective-permute-start | bytes 20744 | tf_op jit(solution)/shard_map/while/body/eval_jaxpr/ppermute | solution.py:22
  268.4 18.6 %collective-permute-start.1 = (bf16[2,576,384]{2,1,0:T(8,128)(2,1)}, bf16[2,576,384]{2,1,0:T(8,128)(2,1)S(1)}, u32[]{:S(2)}, u32[]{:S(2)}) collective-permute-start(bf16[2,576,384]{2,1,0:T(8,128)(2,1)} %get-tuple-element.389), channel_id=1, source_target_pairs={{0,4},{4,8},{8,12},{12,16},{16,20},{20,24},{24,28},{28,32},{32,36}... | collective-permute-start | bytes 2654216 | tf_op jit(solution)/shard_map/while/body/eval_jaxpr/ppermute | solution.py:22
  292.1 5.1 copy-start.3
  300.3 11.1 %collective-permute-start = (s32[3,576]{1,0:T(4,128)S(1)}, s32[3,576]{1,0:T(4,128)S(1)}, u32[]{:S(2)}, u32[]{:S(2)}) collective-permute-start(s32[3,576]{1,0:T(4,128)S(1)} %get-tuple-element.390), channel_id=1, source_target_pairs={{0,4},{4,8},{8,12},{12,16},{16,20},{20,24},{24,28},{28,32},{32,36}... | collective-permute-start | bytes 20744 | tf_op jit(solution)/shard_map/while/body/eval_jaxpr/ppermute | solution.py:22
  306.1 20.0 %collective-permute-start.1 = (bf16[2,576,384]{2,1,0:T(8,128)(2,1)}, bf16[2,576,384]{2,1,0:T(8,128)(2,1)S(1)}, u32[]{:S(2)}, u32[]{:S(2)}) collective-permute-start(bf16[2,576,384]{2,1,0:T(8,128)(2,1)} %get-tuple-element.389), channel_id=1, source_target_pairs={{0,4},{4,8},{8,12},{12,16},{16,20},{20,24},{24,28},{28,32},{32,36}... | collective-permute-start | bytes 2654216 | tf_op jit(solution)/shard_map/while/body/eval_jaxpr/ppermute | solution.py:22
  331.2 5.1 copy-start.3
  339.5 13.2 %collective-permute-start = (s32[3,576]{1,0:T(4,128)S(1)}, s32[3,576]{1,0:T(4,128)S(1)}, u32[]{:S(2)}, u32[]{:S(2)}) collective-permute-start(s32[3,576]{1,0:T(4,128)S(1)} %get-tuple-element.390), channel_id=1, source_target_pairs={{0,4},{4,8},{8,12},{12,16},{16,20},{20,24},{24,28},{28,32},{32,36}... | collective-permute-start | bytes 20744 | tf_op jit(solution)/shard_map/while/body/eval_jaxpr/ppermute | solution.py:22
  345.6 25.0 %collective-permute-start.1 = (bf16[2,576,384]{2,1,0:T(8,128)(2,1)}, bf16[2,576,384]{2,1,0:T(8,128)(2,1)S(1)}, u32[]{:S(2)}, u32[]{:S(2)}) collective-permute-start(bf16[2,576,384]{2,1,0:T(8,128)(2,1)} %get-tuple-element.389), channel_id=1, source_target_pairs={{0,4},{4,8},{8,12},{12,16},{16,20},{20,24},{24,28},{28,32},{32,36}... | collective-permute-start | bytes 2654216 | tf_op jit(solution)/shard_map/while/body/eval_jaxpr/ppermute | solution.py:22
  375.7 5.1 copy-start.3
  383.9 12.8 %collective-permute-start = (s32[3,576]{1,0:T(4,128)S(1)}, s32[3,576]{1,0:T(4,128)S(1)}, u32[]{:S(2)}, u32[]{:S(2)}) collective-permute-start(s32[3,576]{1,0:T(4,128)S(1)} %get-tuple-element.390), channel_id=1, source_target_pairs={{0,4},{4,8},{8,12},{12,16},{16,20},{20,24},{24,28},{28,32},{32,36}... | collective-permute-start | bytes 20744 | tf_op jit(solution)/shard_map/while/body/eval_jaxpr/ppermute | solution.py:22
  391.1 25.1 %collective-permute-start.1 = (bf16[2,576,384]{2,1,0:T(8,128)(2,1)}, bf16[2,576,384]{2,1,0:T(8,128)(2,1)S(1)}, u32[]{:S(2)}, u32[]{:S(2)}) collective-permute-start(bf16[2,576,384]{2,1,0:T(8,128)(2,1)} %get-tuple-element.389), channel_id=1, source_target_pairs={{0,4},{4,8},{8,12},{12,16},{16,20},{20,24},{24,28},{28,32},{32,36}... | collective-permute-start | bytes 2654216 | tf_op jit(solution)/shard_map/while/body/eval_jaxpr/ppermute | solution.py:22
  421.3 5.1 copy-start.3
  429.6 11.1 %collective-permute-start = (s32[3,576]{1,0:T(4,128)S(1)}, s32[3,576]{1,0:T(4,128)S(1)}, u32[]{:S(2)}, u32[]{:S(2)}) collective-permute-start(s32[3,576]{1,0:T(4,128)S(1)} %get-tuple-element.390), channel_id=1, source_target_pairs={{0,4},{4,8},{8,12},{12,16},{16,20},{20,24},{24,28},{28,32},{32,36}... | collective-permute-start | bytes 20744 | tf_op jit(solution)/shard_map/while/body/eval_jaxpr/ppermute | solution.py:22
  435.7 23.6 %collective-permute-start.1 = (bf16[2,576,384]{2,1,0:T(8,128)(2,1)}, bf16[2,576,384]{2,1,0:T(8,128)(2,1)S(1)}, u32[]{:S(2)}, u32[]{:S(2)}) collective-permute-start(bf16[2,576,384]{2,1,0:T(8,128)(2,1)} %get-tuple-element.389), channel_id=1, source_target_pairs={{0,4},{4,8},{8,12},{12,16},{16,20},{20,24},{24,28},{28,32},{32,36}... | collective-permute-start | bytes 2654216 | tf_op jit(solution)/shard_map/while/body/eval_jaxpr/ppermute | solution.py:22
  464.4 5.1 copy-start.3
  472.7 8.0 %collective-permute-start = (s32[3,576]{1,0:T(4,128)S(1)}, s32[3,576]{1,0:T(4,128)S(1)}, u32[]{:S(2)}, u32[]{:S(2)}) collective-permute-start(s32[3,576]{1,0:T(4,128)S(1)} %get-tuple-element.390), channel_id=1, source_target_pairs={{0,4},{4,8},{8,12},{12,16},{16,20},{20,24},{24,28},{28,32},{32,36}... | collective-permute-start | bytes 20744 | tf_op jit(solution)/shard_map/while/body/eval_jaxpr/ppermute | solution.py:22
  478.2 22.2 %collective-permute-start.1 = (bf16[2,576,384]{2,1,0:T(8,128)(2,1)}, bf16[2,576,384]{2,1,0:T(8,128)(2,1)S(1)}, u32[]{:S(2)}, u32[]{:S(2)}) collective-permute-start(bf16[2,576,384]{2,1,0:T(8,128)(2,1)} %get-tuple-element.389), channel_id=1, source_target_pairs={{0,4},{4,8},{8,12},{12,16},{16,20},{20,24},{24,28},{28,32},{32,36}... | collective-permute-start | bytes 2654216 | tf_op jit(solution)/shard_map/while/body/eval_jaxpr/ppermute | solution.py:22
  505.5 5.1 copy-start.3
  513.7 6.2 collective-permute-start
  517.6 21.5 %collective-permute-start.1 = (bf16[2,576,384]{2,1,0:T(8,128)(2,1)}, bf16[2,576,384]{2,1,0:T(8,128)(2,1)S(1)}, u32[]{:S(2)}, u32[]{:S(2)}) collective-permute-start(bf16[2,576,384]{2,1,0:T(8,128)(2,1)} %get-tuple-element.389), channel_id=1, source_target_pairs={{0,4},{4,8},{8,12},{12,16},{16,20},{20,24},{24,28},{28,32},{32,36}... | collective-permute-start | bytes 2654216 | tf_op jit(solution)/shard_map/while/body/eval_jaxpr/ppermute | solution.py:22
  544.1 5.1 copy-start.3
  (39 other events, 127.4 us)
Sparse Core Ops, SparseCore 0:
  9.8 43.9 all-gather.1
  557.6 89.5 reduce-scatter.1
where the time goes:
time: 660 us; the launch traced here: 654 us
  waiting for transfers between devices  222 us (34%)
  blocking collectives  156 us (24%)
  starting transfers between devices  84 us (13%)
  local copies, waits for them, and re-layouts  71.3 us (11%)
  matrix products  60.9 us (9%)
  other arithmetic  45 us (7%)
  between operations  14.4 us (2%)
    psum x2, blocking collectives, from_root(): return lax.psum(kept, axis)  156 us
    ppermute x16, waiting for transfers between devices, from_behind(): return lax.ppermute(value, axis, pairs)  119 us
    reduce_scatter x1, waiting for transfers between devices, shards(): lax.psum_scatter(partial_value.astype(jnp.bfloat16), 'tp', scatter_dimens...  89.7 us
    ppermute x16, starting transfers between devices, from_behind(): return lax.ppermute(value, axis, pairs)  83.9 us
    dot_general x10, matrix products, attend(): jnp.einsum('qhd,khd->hqk', query, kblk, preferred_element_type=jnp.float32)  28.1 us
    slice x17, local copies, waits for them, and re-layouts, attend(): vblk = block[1].reshape(count, heads_local, depth)  25.2 us
    dot_general x10, matrix products, attend(): jnp.einsum('hqk,khd->hqd', weights.astype(jnp.bfloat16), vblk, preferred_...  19.8 us
    slice x8, local copies, waits for them, and re-layouts, attend(): kblk = block[0].reshape(count, heads_local, depth)  16 us
  transfers between devices with their start and end apart: 18, of which 10 were waited for; matrix products, arithmetic and copies ran while one was open for 5% of the time, Pallas kernels for 0%

commit v1 on v0

v1 whole, which is shorter than its diff:
```python
import functools
import math

import jax
import jax.numpy as jnp
from jax import lax
from jax.experimental import pallas as pl
from jax.experimental.pallas import tpu as pltpu
from jax.sharding import PartitionSpec as P

WINDOW = 4096
SINKS = 4
EPS = 1e-05
THETA = 10000.0
LONG = 32832

ROWS = 576
MODEL = 3072
PART = 768
WIDTH = 384
HD = 96
PAD = 128
GROUP = 2304
TILE = 256
CHUNK = 144
STEPS = 4
PREV1 = GROUP
OWN = 2 * GROUP
SINK_AT = 3 * GROUP
SPAN = 3 * GROUP + 16
FAR = 512
NEG = -1e30
MESH = pl.DeviceIdType.MESH
ANY = pl.BlockSpec(memory_space=pl.ANY)
VM = pl.BlockSpec(memory_space=pltpu.VMEM)


def place():
    seq = lax.axis_index("seq")
    tp = lax.axis_index("tp")
    return seq, tp, tp // 2, tp % 2


def remote(src, dst, send, recv, seq, tp):
    return pltpu.make_async_remote_copy(
        src_ref=src,
        dst_ref=dst,
        send_sem=send,
        recv_sem=recv,
        device_id=(seq, tp),
        device_id_type=MESH,
    )


def greet(seq, tp):
    pl.semaphore_signal(
        pltpu.get_barrier_semaphore(), inc=1, device_id=(seq, tp), device_id_type=MESH
    )


def lanes(rows):
    return lax.broadcasted_iota(jnp.int32, (rows, PAD), 1)


def project_kernel(
    x_ref, gain_ref, w_ref, cos_ref, sin_ref, kmark_ref, qmark_ref, sink_ref,
    q_ref, kv_ref, cache_ref,
    held, weights, acc, square, wsem, xsem, send, recv,
):
    seq, tp, yl, core = place()
    mate = yl * 2 + 1 - core
    cross = (1 - yl) * 2 + core
    far = (1 - yl) * 2 + 1 - core
    order = (tp, mate, cross, far)
    own = pltpu.make_async_copy(x_ref, held.at[0], xsem)
    own.start()

    def weight_copy(k):
        start = pl.multiple_of(order[k] * PART, PART)
        return pltpu.make_async_copy(
            w_ref.at[:, pl.ds(start, PART), :], weights.at[k], wsem.at[k]
        )

    for k in range(4):
        weight_copy(k).start()
    greet(seq, mate)
    greet(seq, cross)
    pl.semaphore_wait(pltpu.get_barrier_semaphore(), 2)

    def part(c):
        return pl.ds(c * CHUNK, CHUNK)

    to_cross = [
        remote(x_ref.at[part(c)], held.at[2, part(c)], send.at[c], recv.at[c], seq, cross)
        for c in range(STEPS)
    ]
    for copy in to_cross:
        copy.start()
    to_mate = remote(x_ref, held.at[1], send.at[8], recv.at[8], seq, mate)
    to_mate.start()

    def block(k):
        @pl.loop(0, STEPS)
        def _(c):
            rows = pl.ds(pl.multiple_of(c * CHUNK, CHUNK), CHUNK)
            x = held[k, rows, :].astype(jnp.float32)
            sums = jnp.sum(x * x, axis=-1, keepdims=True)
            y = (x * gain_ref[order[k]]).astype(jnp.bfloat16)
            if k == 0:
                square[rows, :] = sums
            else:
                square[rows, :] += sums
            for j in range(3):
                cols = pl.ds(j * WIDTH, WIDTH)
                term = jnp.dot(y, weights[k, j], preferred_element_type=jnp.float32)
                if k == 0:
                    acc[rows, cols] = term
                else:
                    acc[rows, cols] += term

    own.wait()
    weight_copy(0).wait()
    block(0)
    to_mate.wait_recv()
    weight_copy(1).wait()
    block(1)
    onward = []
    for c in range(STEPS):
        to_cross[c].wait_recv()
        copy = remote(
            held.at[2, part(c)], held.at[3, part(c)], send.at[4 + c], recv.at[4 + c], seq, mate
        )
        copy.start()
        onward.append(copy)
    weight_copy(2).wait()
    block(2)
    for c in range(STEPS):
        onward[c].wait_recv()
    weight_copy(3).wait()
    block(3)

    @pl.loop(0, STEPS)
    def _(c):
        rows = pl.ds(pl.multiple_of(c * CHUNK, CHUNK), CHUNK)
        lane = lanes(CHUNK)
        factor = lax.rsqrt(square[rows, :] / MODEL + EPS)
        kmark = kmark_ref[rows, :]
        qmark = qmark_ref[rows, :]
        valid = 1.0 - kmark[:, 100:101]
        cosine = cos_ref[rows, :]
        sine = sin_ref[rows, :]

        def heads(j):
            b = [acc[rows, pl.ds(j * WIDTH + n * PAD, PAD)] * factor for n in range(3)]
            return b, [
                b[0],
                jnp.where(lane < 32, pltpu.roll(b[0], 32, 1), pltpu.roll(b[1], 32, 1)),
                jnp.where(lane < 64, pltpu.roll(b[1], 64, 1), pltpu.roll(b[2], 64, 1)),
                pltpu.roll(b[2], 96, 1),
            ]

        def turn(u):
            other = jnp.where(lane < 48, pltpu.roll(u, 80, 1), pltpu.roll(u, 48, 1))
            return jnp.where(lane < HD, u * cosine + other * sine, 0.0)

        for h, u in enumerate(heads(0)[1]):
            full = turn(u) * (HD ** -0.5 / math.log(2.0)) + qmark + sink_ref[h]
            q_ref[h, rows, :] = full.astype(jnp.bfloat16)
        keys = []
        for h, u in enumerate(heads(1)[1]):
            k = turn(u)
            keys.append(k)
            kv_ref[h, rows, 0:PAD] = (k + kmark).astype(jnp.bfloat16)
        k1, k2, k3 = (pltpu.roll(keys[1], 96, 1), pltpu.roll(keys[2], 64, 1), pltpu.roll(keys[3], 32, 1))
        joined = (
            jnp.where(lane < 96, keys[0], k1),
            jnp.where(lane < 64, k1, k2),
            jnp.where(lane < 32, k2, k3),
        )
        plain, values = heads(2)
        for n in range(3):
            cols = pl.ds(n * PAD, PAD)
            cache_ref[0, rows, cols] = (joined[n] * valid).astype(jnp.bfloat16)
            cache_ref[1, rows, cols] = (plain[n] * valid).astype(jnp.bfloat16)
        for h, u in enumerate(values):
            v = jnp.where(lane < HD, u, jnp.where(lane == HD, 1.0, 0.0))
            kv_ref[h, rows, PAD:] = v.astype(jnp.bfloat16)

    for c in range(STEPS):
        to_cross[c].wait_send()
        onward[c].wait_send()
    to_mate.wait_send()


def exchange_kernel(
    q_ref, kv_ref, wo_ref, qo_ref, kvo_ref, wg_ref,
    a_send, a_recv, x_send, z_send, one_recv, two_recv, s_send, s_recv, w_send, w_recv,
):
    seq, tp, yl, core = place()
    group = seq // 4
    m = seq % 4
    z = seq // 8
    xp = group % 2
    xb = m // 2
    hy = m % 2
    hx = xb + xp - 2 * xp * xb
    mate = yl * 2 + 1 - core
    cross = (1 - yl) * 2 + core
    far = (1 - yl) * 2 + 1 - core
    flipped = seq + 1 - 2 * hy
    beside = 4 * (group + 1 - 2 * xp) + (1 - xb) * 2 + hy
    root = hx * 2 + hy

    def holder(g):
        odd = g % 2
        return 4 * g + (hx + odd - 2 * odd * hx) * 2 + hy

    for d in range(4):
        greet(4 * group + d, cross)
    greet(seq, mate)
    greet(flipped, far)
    greet(beside, tp)

    @pl.when(z > 0)
    def _():
        greet(seq - 8, tp)

    @pl.when(z < 7)
    def _():
        greet(seq + 8, tp)

    @pl.when(group == 0)
    def _():
        @pl.loop(1, 16)
        def _(g):
            greet(holder(g), tp)

    @pl.when(group > 0)
    def _():
        greet(root, tp)

    count = 7 + jnp.where(z > 0, 1, 0) + jnp.where(z < 7, 1, 0) + jnp.where(group == 0, 15, 1)
    pl.semaphore_wait(pltpu.get_barrier_semaphore(), count)

    def own_rows(s):
        return pl.ds(pl.multiple_of(OWN + s * ROWS, 64), ROWS)

    def q_rows(s):
        return pl.ds(pl.multiple_of(s * ROWS, 64), ROWS)

    sends = []
    for d in range(4):
        b = d // 2
        h = (b + xp - 2 * xp * b) * 2 + d % 2
        copy = remote(
            kv_ref.at[h], kvo_ref.at[own_rows(m)], a_send.at[d, 0], a_recv.at[m, 0], 4 * group + d, cross
        )
        copy.start()
        sends.append(copy)
    for d in range(4):
        b = d // 2
        h = (b + xp - 2 * xp * b) * 2 + d % 2
        copy = remote(
            q_ref.at[h], qo_ref.at[q_rows(m)], a_send.at[d, 1], a_recv.at[m, 1], 4 * group + d, cross
        )
        copy.start()
        sends.append(copy)

    def columns(t):
        return pl.ds(pl.multiple_of(t * PART, PART), PART)

    for n, (s2, t2) in enumerate(((seq, mate), (seq, cross), (flipped, far))):
        copy = remote(wo_ref.at[:, columns(t2)], wg_ref.at[n], w_send.at[n], w_recv.at[n], s2, t2)
        copy.start()
        sends.append(copy)

    def arrived(ref, sem):
        pltpu.make_async_copy(ref, ref, sem).wait()

    def tail(s):
        return pl.ds(s * ROWS + (FAR if s == 0 else 0), 64 if s == 0 else ROWS)

    def whole(s):
        return pl.ds(s * ROWS, ROWS)

    def after(s):
        return pl.ds(PREV1 + s * ROWS, ROWS)

    def mine(s):
        return pl.ds(OWN + s * ROWS, ROWS)

    def mine_tail(s):
        return pl.ds(OWN + s * ROWS + (FAR if s == 0 else 0), 64 if s == 0 else ROWS)

    def across(s):
        return remote(kvo_ref.at[mine(s)], kvo_ref.at[after(s)], x_send.at[s], one_recv.at[s], beside, tp)

    def passed(s):
        return remote(kvo_ref.at[whole(s)], kvo_ref.at[after(s)], x_send.at[s], one_recv.at[s], beside, tp)

    def ahead(s):
        return remote(kvo_ref.at[mine(s)], kvo_ref.at[whole(s)], z_send.at[s], two_recv.at[s], seq + 8, tp)

    def ahead_tail(s):
        return remote(
            kvo_ref.at[mine_tail(s)], kvo_ref.at[tail(s)], z_send.at[s], two_recv.at[s], seq + 8, tp
        )

    def sink_copy(g):
        return remote(
            kvo_ref.at[pl.ds(OWN, 16)], kvo_ref.at[pl.ds(SINK_AT, 16)], s_send.at[g], s_recv, holder(g), tp
        )

    for s in range(4):
        arrived(kvo_ref.at[mine(s)], a_recv.at[s, 0])

        @pl.when(xp == 0)
        def _():
            across(s).start()

        if s == 0:
            @pl.when(group == 0)
            def _():
                @pl.loop(1, 16)
                def _(g):
                    sink_copy(g).start()

        @pl.when((xp == 0) & (z < 7))
        def _():
            ahead_tail(s).start()

        @pl.when((xp == 1) & (z < 7))
        def _():
            ahead(s).start()

    @pl.when((xp == 1) & (z > 0))
    def _():
        for s in range(4):
            arrived(kvo_ref.at[whole(s)], two_recv.at[s])
            passed(s).start()

    @pl.when((xp == 0) & (z > 0))
    def _():
        for s in range(4):
            arrived(kvo_ref.at[tail(s)], two_recv.at[s])

    @pl.when((xp == 1) | (z > 0))
    def _():
        for s in range(4):
            arrived(kvo_ref.at[after(s)], one_recv.at[s])

    @pl.when(group > 0)
    def _():
        arrived(kvo_ref.at[pl.ds(SINK_AT, 16)], s_recv)

    for s in range(4):
        arrived(qo_ref.at[whole(s)], a_recv.at[s, 1])
    for n in range(3):
        arrived(wg_ref.at[n], w_recv.at[n])
    for copy in sends:
        copy.wait_send()

    @pl.when(xp == 0)
    def _():
        for s in range(4):
            across(s).wait_send()

    @pl.when((xp == 1) & (z > 0))
    def _():
        for s in range(4):
            passed(s).wait_send()

    @pl.when((xp == 0) & (z < 7))
    def _():
        for s in range(4):
            ahead_tail(s).wait_send()

    @pl.when((xp == 1) & (z < 7))
    def _():
        for s in range(4):
            ahead(s).wait_send()

    @pl.when(group == 0)
    def _():
        @pl.loop(1, 16)
        def _(g):
            sink_copy(g).wait_send()


def dot_t(a, b):
    return lax.dot_general(a, b, (((1,), (1,)), ((), ())), preferred_element_type=jnp.float32)


def attend_kernel(q_ref, kvh_ref, o_ref, kv, scores, sem):
    seq = lax.axis_index("seq")
    group = seq // 4

    def load(start, size, n):
        return pltpu.make_async_copy(
            kvh_ref.at[pl.ds(start, size)], kv.at[pl.ds(start, size)], sem.at[n]
        )

    def blank(start, size):
        mark = lax.broadcasted_iota(jnp.int32, (16, 2 * PAD), 1)
        row = jnp.where(mark == 102, 1.0, 0.0).astype(jnp.bfloat16)

        @pl.loop(0, size // 16)
        def _(n):
            kv[pl.ds(pl.multiple_of(start + n * 16, 16), 16), :] = row

    pieces = ((OWN, GROUP, 0), (PREV1, GROUP, 1), (FAR, GROUP - FAR, 2), (SINK_AT, 16, 1))
    for n, (start, size, least) in enumerate(pieces):
        @pl.when(group >= least)
        def _():
            load(start, size, n).start()

        @pl.when(group < least)
        def _():
            blank(start, size)

    for n, (start, size, least) in enumerate(pieces):
        @pl.when(group >= least)
        def _():
            load(start, size, n).wait()

    def key(start, size):
        return kv[pl.ds(pl.multiple_of(start, TILE), size), 0:PAD]

    def val(start, size):
        return kv[pl.ds(pl.multiple_of(start, TILE), size), PAD:]

    down = lax.broadcasted_iota(jnp.int32, (TILE, TILE), 0)
    right = lax.broadcasted_iota(jnp.int32, (TILE, TILE), 1)
    lower = right <= down
    sink_k = kv[pl.ds(SINK_AT, 16), 0:PAD]
    sink_v = kv[pl.ds(SINK_AT, 16), PAD:]
    small_down = lax.broadcasted_iota(jnp.int32, (TILE, 16), 0)
    small_right = lax.broadcasted_iota(jnp.int32, (TILE, 16), 1)

    def finish(rows, acc):
        lane = lanes(TILE)
        out = acc * (1.0 / acc[:, HD:HD + 1])
        o_ref[rows, :] = jnp.where(lane < HD, out, 0.0).astype(jnp.bfloat16)

    def long_tile(i, rows, first):
        q = q_ref[rows, :]
        near = OWN + i * TILE
        outer = FAR + i * TILE
        s = jnp.where(lower, dot_t(q, key(near, TILE)), dot_t(q, key(outer, TILE)))
        scores[:, 0:TILE] = s
        top = jnp.maximum(s[:, :PAD], s[:, PAD:])
        distance = first + small_down - small_right
        seen = (small_right < SINKS) & (distance >= WINDOW)
        sink_s = jnp.where(seen, dot_t(q, sink_k), NEG)
        for c in range(5):
            s = dot_t(q, key(outer + TILE + c * 768, 768))
            scores[:, pl.ds(TILE + c * 768, 768)] = s
            for n in range(6):
                top = jnp.maximum(top, s[:, n * PAD:(n + 1) * PAD])
        peak = jnp.maximum(
            jnp.max(top, axis=-1, keepdims=True), jnp.max(sink_s, axis=-1, keepdims=True)
        )
        w = jnp.where(seen, jnp.exp2(sink_s - peak), 0.0).astype(jnp.bfloat16)
        acc = jnp.dot(w, sink_v, preferred_element_type=jnp.float32)
        w = jnp.exp2(scores[:, 0:TILE] - peak)
        acc += jnp.dot(
            jnp.where(lower, w, 0.0).astype(jnp.bfloat16), val(near, TILE), preferred_element_type=jnp.float32
        )
        acc += jnp.dot(
            jnp.where(lower, 0.0, w).astype(jnp.bfloat16), val(outer, TILE), preferred_element_type=jnp.float32
        )
        for c in range(5):
            w = jnp.exp2(scores[:, pl.ds(TILE + c * 768, 768)] - peak).astype(jnp.bfloat16)
            acc += jnp.dot(w, val(outer + TILE + c * 768, 768), preferred_element_type=jnp.float32)
        finish(rows, acc)

    def mixed_tile(i, rows, first):
        q = q_ref[rows, :]
        lane = lanes(TILE)
        qf = q.astype(jnp.float32)
        mine = qf[:, 101:102]
        pick = jnp.where(lane == 96, -1.0, jnp.where(lane == 97, mine, 0.0)).astype(jnp.bfloat16)
        lost = jnp.where(lane == 100, 1.0, 0.0).astype(jnp.bfloat16)
        distance = first + small_down - small_right
        seen = (small_right < SINKS) & (distance >= WINDOW) & (dot_t(pick, sink_k) == 0.0)
        sink_s = jnp.where(seen, dot_t(q, sink_k), NEG)
        peak = jnp.max(sink_s, axis=-1, keepdims=True)
        w = jnp.where(seen, jnp.exp2(sink_s - peak), 0.0).astype(jnp.bfloat16)
        acc = jnp.dot(w, sink_v, preferred_element_type=jnp.float32)
        low = jnp.where(first >= LONG, 15, 0)

        def step(n, carry):
            peak, acc = carry
            start = FAR + i * TILE + n * TILE
            k = key(start, TILE)
            gap = (16 - n) * TILE + down - right
            bad = dot_t(lost, k)
            seen = (gap >= 0) & (gap < WINDOW) & (dot_t(pick, k) == 0.0) & ((bad < 0.5) | (gap == 0))
            s = jnp.where(seen, dot_t(q, k), NEG)
            now = jnp.maximum(peak, jnp.max(s, axis=-1, keepdims=True))
            w = jnp.where(seen, jnp.exp2(s - now), 0.0).astype(jnp.bfloat16)
            acc = acc * jnp.exp2(peak - now) + jnp.dot(w, val(start, TILE), preferred_element_type=jnp.float32)
            return now, acc

        peak, acc = lax.fori_loop(low, 17, step, (peak, acc))
        finish(rows, acc)

    @pl.loop(0, GROUP // TILE)
    def _(i):
        rows = pl.ds(pl.multiple_of(i * TILE, TILE), TILE)
        first = group * GROUP + i * TILE

        @pl.when(first + TILE <= LONG)
        def _():
            long_tile(i, rows, first)

        @pl.when(first + TILE > LONG)
        def _():
            mixed_tile(i, rows, first)


def gather_kernel(o_ref, mg_ref, send, recv, lsem):
    seq, tp, yl, core = place()
    group = seq // 4
    m = seq % 4
    xp = group % 2
    mate = yl * 2 + 1 - core
    partner = core + 1 - 2 * core

    def head(member, low, who):
        b = member // 2
        return 4 * ((1 - low) * 2 + who) + (b + xp - 2 * xp * b) * 2 + member % 2

    mine = head(m, yl, core)
    greet(seq, mate)
    for d in range(4):
        for low in range(2):
            @pl.when((m != d) | (yl != low))
            def _():
                greet(4 * group + d, low * 2 + core)
    pl.semaphore_wait(pltpu.get_barrier_semaphore(), 8)

    def out(d, low):
        return remote(
            o_ref.at[pl.ds(d * ROWS, ROWS)], mg_ref.at[mine],
            send.at[d * 2 + low], recv.at[mine], 4 * group + d, low * 2 + core,
        )

    def local(d):
        return pltpu.make_async_copy(o_ref.at[pl.ds(d * ROWS, ROWS)], mg_ref.at[mine], lsem)

    def onward(d, low):
        g = head(d, low, core)
        return remote(mg_ref.at[g], mg_ref.at[g], send.at[8 + d * 2 + low], recv.at[g], seq, mate)

    def arrived(g):
        pltpu.make_async_copy(mg_ref.at[g], mg_ref.at[g], recv.at[g]).wait()

    for d in range(4):
        for low in range(2):
            @pl.when((m != d) | (yl != low))
            def _():
                out(d, low).start()

            @pl.when((m == d) & (yl == low))
            def _():
                local(d).start()

    for d in range(4):
        for low in range(2):
            @pl.when((m != d) | (yl != low))
            def _():
                arrived(head(d, low, core))

            @pl.when((m == d) & (yl == low))
            def _():
                local(d).wait()

            onward(d, low).start()
    for d in range(4):
        for low in range(2):
            arrived(head(d, low, partner))
    for d in range(4):
        for low in range(2):
            @pl.when((m != d) | (yl != low))
            def _():
                out(d, low).wait_send()

            onward(d, low).wait_send()


def output_kernel(mg_ref, wo_ref, wg_ref, y_ref, own, padded, sem):
    seq, tp, yl, core = place()
    order = (tp, yl * 2 + 1 - core, (1 - yl) * 2 + core, (1 - yl) * 2 + 1 - core)
    copy = pltpu.make_async_copy(wo_ref.at[:, pl.ds(pl.multiple_of(tp * PART, PART), PART)], own, sem)
    copy.start()
    for n in range(16):
        padded[pl.ds(n * PAD + HD, PAD - HD), :] = jnp.zeros((PAD - HD, PART), jnp.bfloat16)
    for n in range(12):
        padded[pl.ds((n + 4) * PAD, HD), :] = wg_ref[n // 4, pl.ds(n % 4 * HD, HD), :]
    copy.wait()
    for n in range(4):
        padded[pl.ds(n * PAD, HD), :] = own[pl.ds(n * HD, HD), :]

    @pl.loop(0, STEPS)
    def _(c):
        rows = pl.ds(pl.multiple_of(c * CHUNK, CHUNK), CHUNK)
        left = jnp.concatenate(
            [mg_ref[4 * order[n // 4] + n % 4, rows, :] for n in range(16)], axis=1
        )
        y_ref[rows, :] = jnp.dot(left, padded[...], preferred_element_type=jnp.float32).astype(jnp.bfloat16)


def shards(tokens, norm_gain, w_qkv, w_out, sink_logit, segment_ids, positions, padding_mask):
    bf16, f32 = jnp.bfloat16, jnp.float32
    spot = jnp.arange(PAD, dtype=jnp.int32)
    freq = THETA ** (-((spot % 48).astype(f32) * 2.0 / HD))
    angle = positions.astype(f32)[:, None] * freq[None, :]
    cosine = jnp.cos(angle)
    sine = jnp.where(spot[None, :] < 48, -jnp.sin(angle), jnp.sin(angle))
    seg = segment_ids.astype(f32)[:, None]
    sinkish = (positions < SINKS).astype(f32)[:, None]
    lost = 1.0 - padding_mask.astype(f32)[:, None]
    kmark = jnp.where(spot == 96, seg, 0.0) + jnp.where(spot == 97, 1.0, 0.0)
    kmark = kmark + jnp.where((spot == 98) | (spot == 99), sinkish, 0.0) + jnp.where(spot == 100, lost, 0.0)
    qmark = jnp.where(spot == 101, seg, 0.0) + jnp.where(spot == 102, NEG, 0.0)
    logit = sink_logit * (1.0 / math.log(2.0))
    high = lax.reduce_precision(logit, 8, 7)
    low = logit - high
    sink = jnp.where(spot == 98, high[:, None], 0.0) + jnp.where(spot == 99, low[:, None], 0.0)
    sink = sink.reshape(4, 1, PAD)

    dma = pltpu.SemaphoreType.DMA
    q, kv, cache = pl.pallas_call(
        project_kernel,
        out_shape=(
            jax.ShapeDtypeStruct((4, ROWS, PAD), bf16),
            jax.ShapeDtypeStruct((4, ROWS, 2 * PAD), bf16),
            jax.ShapeDtypeStruct((2, ROWS, WIDTH), bf16),
        ),
        in_specs=[ANY, VM, ANY, VM, VM, VM, VM, VM],
        out_specs=(VM, VM, VM),
        scratch_shapes=[
            pltpu.VMEM((4, ROWS, PART), bf16),
            pltpu.VMEM((4, 3, PART, WIDTH), bf16),
            pltpu.VMEM((ROWS, 3 * WIDTH), f32),
            pltpu.VMEM((ROWS, 1), f32),
            dma((4,)),
            dma,
            dma((9,)),
            dma((9,)),
        ],
        compiler_params=pltpu.CompilerParams(collective_id=0, has_side_effects=True),
        name="project",
    )(
        tokens, norm_gain.reshape(4, 1, PART), jnp.transpose(w_qkv, (1, 0, 2)),
        cosine, sine, kmark, qmark, sink,
    )
    qo, kvo, wg = pl.pallas_call(
        exchange_kernel,
        out_shape=(
            jax.ShapeDtypeStruct((GROUP, PAD), bf16),
            jax.ShapeDtypeStruct((SPAN, 2 * PAD), bf16),
            jax.ShapeDtypeStruct((3, WIDTH, PART), bf16),
        ),
        in_specs=[ANY, ANY, ANY],
        out_specs=(ANY, ANY, ANY),
        scratch_shapes=[
            dma((4, 2)), dma((4, 2)), dma((4,)), dma((4,)), dma((4,)), dma((4,)),
            dma((16,)), dma, dma((3,)), dma((3,)),
        ],
        compiler_params=pltpu.CompilerParams(collective_id=1, has_side_effects=True),
        name="exchange",
    )(q, kv, w_out)
    mixed = pl.pallas_call(
        attend_kernel,
        out_shape=jax.ShapeDtypeStruct((GROUP, PAD), bf16),
        in_specs=[VM, ANY],
        out_specs=VM,
        scratch_shapes=[
            pltpu.VMEM((SPAN, 2 * PAD), bf16),
            pltpu.VMEM((TILE, WINDOW), f32),
            dma((4,)),
        ],
        name="attend",
    )(qo, kvo)
    mg = pl.pallas_call(
        gather_kernel,
        out_shape=jax.ShapeDtypeStruct((16, ROWS, PAD), bf16),
        in_specs=[VM],
        out_specs=ANY,
        scratch_shapes=[dma((16,)), dma((16,)), dma],
        compiler_params=pltpu.CompilerParams(collective_id=2, has_side_effects=True),
        name="gather",
    )(mixed)
    y = pl.pallas_call(
        output_kernel,
        out_shape=jax.ShapeDtypeStruct((ROWS, PART), bf16),
        in_specs=[VM, ANY, VM],
        out_specs=VM,
        scratch_shapes=[
            pltpu.VMEM((WIDTH, PART), bf16),
            pltpu.VMEM((16 * PAD, PART), bf16),
            dma,
        ],
        name="output",
    )(mg, w_out, wg)
    return (y, cache)


def solution(mesh):
    return jax.shard_map(
        shards,
        mesh=mesh,
        in_specs=(
            P("seq", "tp"),
            P(),
            P(None, None, "tp"),
            P("tp", None),
            P("tp"),
            P("seq"),
            P("seq"),
            P("seq"),
        ),
        out_specs=(P("seq", "tp"), P(None, "seq", "tp")),
        check_vma=False,
    )
```

time: 660 us -> 154 us (0.23)
  waiting for transfers between devices: 222 us -> 0 us
  blocking collectives: 156 us -> 0 us
  Pallas kernels: 0 us -> 145 us
  starting transfers between devices: 84 us -> 0 us
  local copies, waits for them, and re-layouts: 71.3 us -> 0.92 us
  matrix products: 60.9 us -> 0 us
  other arithmetic: 45 us -> 7.13 us
  between operations: 14.4 us -> 0.71 us
    psum x2 -> x0, blocking collectives: 156 us -> none  [from_root(): return lax.psum(kept, axis)]
    pallas_call x0 -> x5, Pallas kernels: none -> 145 us  [the longest x1 51.8 us: shards(): pl.pallas_call(exchange_kernel, out_shape=(jax.ShapeDtypeStruct((GROUP, P...]
    ppermute x16 -> x0, waiting for transfers between devices: 119 us -> none  [from_behind(): return lax.ppermute(value, axis, pairs)]
    reduce_scatter x1 -> x0, waiting for transfers between devices: 89.7 us -> none  [shards(): lax.psum_scatter(partial_value.astype(jnp.bfloat16), 'tp', scatter_dimens...]
    ppermute x16 -> x0, starting transfers between devices: 83.9 us -> none  [from_behind(): return lax.ppermute(value, axis, pairs)]
    dot_general x22 -> x0, matrix products: 60.9 us -> none  [the longest x10 28.1 us: attend(): jnp.einsum('qhd,khd->hqk', query, kblk, preferred_element_type=jnp.float32)]
    slice x35 -> x0, local copies, waits for them, and re-layouts: 42.2 us -> none  [the longest x17 25.2 us: attend(): vblk = block[1].reshape(count, heads_local, depth)]
    reduce_sum x11 -> x0, other arithmetic: 18.5 us -> none  [the longest x10 15.7 us: attend(): total = total * fade + jnp.sum(weights, axis=-1)]
  transfers between devices with their start and end apart: 18 -> 0, of which waited for: 10 -> 0; matrix products, arithmetic and copies ran while one was open for 5% -> 0% of each run, Pallas kernels for 0% -> 0%
where the time goes in v1:
time: 154 us
  Pallas kernels  145 us (94%)
  other arithmetic  7.13 us (5%)
    pallas_call x1, Pallas kernels, shards(): pl.pallas_call(exchange_kernel, out_shape=(jax.ShapeDtypeStruct((GROUP, P...  51.8 us
    pallas_call x1, Pallas kernels, shards(): pl.pallas_call(project_kernel, out_shape=(jax.ShapeDtypeStruct((4, ROWS,...  31.8 us
    pallas_call x1, Pallas kernels, shards(): pl.pallas_call(attend_kernel, out_shape=jax.ShapeDtypeStruct((GROUP, PAD)...  30.5 us
    pallas_call x1, Pallas kernels, shards(): pl.pallas_call(gather_kernel, out_shape=jax.ShapeDtypeStruct((16, ROWS, P...  24.2 us
    pallas_call x1, Pallas kernels, shards(): pl.pallas_call(output_kernel, out_shape=jax.ShapeDtypeStruct((ROWS, PART)...  6.94 us

profile of v1, /device:TPU:241, one launch (start us, length us, event | category | flops | bytes accessed | tf_op | source)
XLA Modules:
  0.0 154.1 jit_solution(8376318312088790978)
XLA Ops:
  0.7 0.7 multiply_reduce-precision_fusion
  1.3 0.7 fusion.sink_ref
  2.0 0.7 convert_element_type.21
  2.7 0.7 convert_subtract_fusion
  3.4 0.7 compare_convert_fusion
  4.1 0.7 convert_element_type.19
  4.8 1.1 select_add_fusion
  5.8 1.9 %negate_select_fusion = (f32[576,128]{1,0:T(8,128)}, f32[576,128]{1,0:T(8,128)}) fusion(f32[128]{0:T(128)S(1)} %fusion.4, f32[576]{0:T(1024)S(1)} %convert_element_type.19, pred[128]{0:T(512)(128)(4,1)S(1)} %iota_compare_fusion.5), kind=kLoop, calls=%fused_computation | loop fusion | flops 221184 | bytes 592768 | tf_op jit(solution)/shard_map/jit(_where)/select_n | solution.py:620
  7.8 31.8 %project.1 = (bf16[4,576,128]{2,1,0:T(8,128)(2,1)}, bf16[4,576,256]{2,1,0:T(8,128)(2,1)}, bf16[2,576,384]{2,1,0:T(8,128)(2,1)}) custom-call(bf16[576,768]{1,0:T(8,128)(2,1)} %x_ref.1, f32[4,1,768]{2,1,0:T(1,128)} %bitcast.3, bf16[3,3072,384]{2,1,0:T(8,128)(2,1)} %bitcast.2, f32[576,128]{1,0:T(8,128)} %get-tuple-element.15.cos_ref, ...), custom_call_target="tpu_custom_call" | custom-call | tf_op jit(solution)/shard_map/project/pallas_call | solution.py:634
  39.6 51.8 %exchange.1 = (bf16[2304,128]{1,0:T(8,128)(2,1)}, bf16[6928,256]{1,0:T(8,128)(2,1)}, bf16[3,384,768]{2,1,0:T(8,128)(2,1)}) custom-call(bf16[4,576,128]{2,1,0:T(8,128)(2,1)} %get-tuple-element.8.q_ref, bf16[4,576,256]{2,1,0:T(8,128)(2,1)} %get-tuple-element.9.kv_ref, bf16[384,3072]{1,0:T(8,128)(2,1)} %wo_ref.3), custom_call_target="tpu_custom_call" | custom-call | tf_op jit(solution)/shard_map/exchange/pallas_call | solution.py:659
  91.4 30.5 %attend.1.o_ref = bf16[2304,128]{1,0:T(8,128)(2,1)} custom-call(bf16[2304,128]{1,0:T(8,128)(2,1)} %get-tuple-element.10.q_ref, bf16[6928,256]{1,0:T(8,128)(2,1)} %get-tuple-element.11.kvh_ref), custom_call_target="tpu_custom_call" | custom-call | tf_op jit(solution)/shard_map/attend/pallas_call | solution.py:675
  122.0 24.2 %gather.1.mg_ref = bf16[16,576,128]{2,1,0:T(8,128)(2,1)} custom-call(bf16[2304,128]{1,0:T(8,128)(2,1)} %attend.1.o_ref), custom_call_target="tpu_custom_call" | custom-call | tf_op jit(solution)/shard_map/gather/pallas_call | solution.py:687
  146.2 0.0 copy-start
  146.2 6.9 %output.1 = bf16[576,768]{1,0:T(8,128)(2,1)} custom-call(bf16[16,576,128]{2,1,0:T(8,128)(2,1)} %gather.1.mg_ref, bf16[384,3072]{1,0:T(8,128)(2,1)} %wo_ref.3, bf16[3,384,768]{2,1,0:T(8,128)(2,1)} %get-tuple-element.12.wg_ref), custom_call_target="tpu_custom_call" | custom-call | tf_op jit(solution)/shard_map/output/pallas_call | solution.py:696
  153.1 0.0 copy-done
  153.1 0.9 copy.11
  (6 shorter events, 0.0 us)
Async XLA Ops:
  146.2 7.0 %copy-start = (bf16[2,576,384]{2,1,0:T(8,128)(2,1)S(1)}, bf16[2,576,384]{2,1,0:T(8,128)(2,1)}, u32[]{:S(2)}) copy-start(bf16[2,576,384]{2,1,0:T(8,128)(2,1)} %get-tuple-element.31) | copy-start | bytes 2654212

commit v2 on v1

v2 whole, which is shorter than its diff:
```python
import functools
import math

import jax
import jax.numpy as jnp
from jax import lax
from jax.experimental import pallas as pl
from jax.experimental.pallas import tpu as pltpu
from jax.sharding import PartitionSpec as P

WINDOW = 4096
SINKS = 4
EPS = 1e-05
THETA = 10000.0
LONG = 32832

ROWS = 576
MODEL = 3072
PART = 768
WIDTH = 384
HD = 96
PAD = 128
GROUP = 2304
TILE = 256
CHUNK = 144
STEPS = 4
PREV1 = GROUP
OWN = 2 * GROUP
SINK_AT = 3 * GROUP
SPAN = 3 * GROUP + 16
FAR = 512
NEG = -1e30
MESH = pl.DeviceIdType.MESH
ANY = pl.BlockSpec(memory_space=pl.ANY)
VM = pl.BlockSpec(memory_space=pltpu.VMEM)


def place():
    seq = lax.axis_index("seq")
    tp = lax.axis_index("tp")
    return seq, tp, tp // 2, tp % 2


def remote(src, dst, send, recv, seq, tp):
    return pltpu.make_async_remote_copy(
        src_ref=src,
        dst_ref=dst,
        send_sem=send,
        recv_sem=recv,
        device_id=(seq, tp),
        device_id_type=MESH,
    )


def greet(seq, tp):
    pl.semaphore_signal(
        pltpu.get_barrier_semaphore(), inc=1, device_id=(seq, tp), device_id_type=MESH
    )


def lanes(rows):
    return lax.broadcasted_iota(jnp.int32, (rows, PAD), 1)


def project_kernel(
    x_ref, gain_ref, w_ref, cos_ref, sin_ref, kmark_ref, qmark_ref, sink_ref, wo_ref,
    q_ref, kv_ref, cache_ref, wg_ref,
    held, weights, acc, square, wsem, xsem, send, recv, wsend, wrecv,
):
    seq, tp, yl, core = place()
    mate = yl * 2 + 1 - core
    cross = (1 - yl) * 2 + core
    far = (1 - yl) * 2 + 1 - core
    flipped = seq + 1 - 2 * (seq % 2)
    order = (tp, mate, cross, far)
    own = pltpu.make_async_copy(x_ref, held.at[0], xsem)
    own.start()

    def weight_copy(k):
        start = pl.multiple_of(order[k] * PART, PART)
        return pltpu.make_async_copy(
            w_ref.at[:, pl.ds(start, PART), :], weights.at[k], wsem.at[k]
        )

    for k in range(4):
        weight_copy(k).start()
    greet(seq, mate)
    greet(seq, cross)
    greet(flipped, cross)
    greet(flipped, far)
    pl.semaphore_wait(pltpu.get_barrier_semaphore(), 4)

    def part(c):
        return pl.ds(pl.multiple_of(c * CHUNK, CHUNK), CHUNK)

    def to_cross(c):
        return remote(x_ref.at[part(c)], held.at[2, part(c)], send.at[c], recv.at[c], seq, cross)

    @pl.loop(0, STEPS)
    def _(c):
        to_cross(c).start()

    to_mate = remote(x_ref, held.at[1], send.at[8], recv.at[8], seq, mate)
    to_mate.start()

    def block(k, c):
        rows = part(c)
        x = held[k, rows, :].astype(jnp.float32)
        sums = jnp.sum(x * x, axis=-1, keepdims=True)
        y = (x * gain_ref[order[k]]).astype(jnp.bfloat16)
        if k == 0:
            square[rows, :] = sums
        else:
            square[rows, :] += sums
        for j in range(3):
            cols = pl.ds(j * WIDTH, WIDTH)
            term = jnp.dot(y, weights[k, j], preferred_element_type=jnp.float32)
            if k == 0:
                acc[rows, cols] = term
            else:
                acc[rows, cols] += term

    def close(c):
        rows = part(c)
        lane = lanes(CHUNK)
        factor = lax.rsqrt(square[rows, :] / MODEL + EPS)
        kmark = kmark_ref[rows, :]
        qmark = qmark_ref[rows, :]
        valid = 1.0 - kmark[:, 100:101]
        cosine = cos_ref[rows, :]
        sine = sin_ref[rows, :]

        def heads(j):
            b = [acc[rows, pl.ds(j * WIDTH + n * PAD, PAD)] * factor for n in range(3)]
            return b, [
                b[0],
                jnp.where(lane < 32, pltpu.roll(b[0], 32, 1), pltpu.roll(b[1], 32, 1)),
                jnp.where(lane < 64, pltpu.roll(b[1], 64, 1), pltpu.roll(b[2], 64, 1)),
                pltpu.roll(b[2], 96, 1),
            ]

        def turn(u):
            other = jnp.where(lane < 48, pltpu.roll(u, 80, 1), pltpu.roll(u, 48, 1))
            return jnp.where(lane < HD, u * cosine + other * sine, 0.0)

        for h, u in enumerate(heads(0)[1]):
            full = turn(u) * (HD ** -0.5 / math.log(2.0)) + qmark + sink_ref[h]
            q_ref[h, rows, :] = full.astype(jnp.bfloat16)
        keys = []
        for h, u in enumerate(heads(1)[1]):
            k = turn(u)
            keys.append(k)
            kv_ref[h, rows, 0:PAD] = (k + kmark).astype(jnp.bfloat16)
        k1, k2, k3 = (pltpu.roll(keys[1], 96, 1), pltpu.roll(keys[2], 64, 1), pltpu.roll(keys[3], 32, 1))
        joined = (
            jnp.where(lane < 96, keys[0], k1),
            jnp.where(lane < 64, k1, k2),
            jnp.where(lane < 32, k2, k3),
        )
        plain, values = heads(2)
        for n in range(3):
            cols = pl.ds(n * PAD, PAD)
            cache_ref[0, rows, cols] = (joined[n] * valid).astype(jnp.bfloat16)
            cache_ref[1, rows, cols] = (plain[n] * valid).astype(jnp.bfloat16)
        for h, u in enumerate(values):
            v = jnp.where(lane < HD, u, jnp.where(lane == HD, 1.0, 0.0))
            kv_ref[h, rows, PAD:] = v.astype(jnp.bfloat16)

    def wide(t):
        return pl.ds(pl.multiple_of(t * PART, PART), PART)

    slabs = [
        remote(wo_ref.at[:, wide(t2)], wg_ref.at[n], wsend.at[n], wrecv.at[n], s2, t2)
        for n, (s2, t2) in enumerate(((seq, mate), (flipped, cross), (flipped, far)))
    ]
    for copy in slabs:
        copy.start()

    own.wait()
    weight_copy(0).wait()

    @pl.loop(0, STEPS)
    def _(c):
        block(0, c)

    to_mate.wait_recv()
    weight_copy(1).wait()

    @pl.loop(0, STEPS)
    def _(c):
        block(1, c)

    weight_copy(2).wait()
    weight_copy(3).wait()

    def onward(c):
        return remote(
            held.at[2, part(c)], held.at[3, part(c)], send.at[4 + c], recv.at[4 + c], seq, mate
        )

    @pl.loop(0, STEPS + 1)
    def _(c):
        @pl.when(c < STEPS)
        def _():
            to_cross(c).wait_recv()
            onward(c).start()
            block(2, c)

        @pl.when(c > 0)
        def _():
            onward(c - 1).wait_recv()
            block(3, c - 1)
            close(c - 1)

    @pl.loop(0, STEPS)
    def _(c):
        to_cross(c).wait_send()
        onward(c).wait_send()

    to_mate.wait_send()
    for copy in slabs:
        copy.wait()


def exchange_kernel(
    q_ref, kv_ref, qo_ref, kvo_ref,
    a_send, a_recv, b_send, b_recv, x_send, z_send, one_recv, two_recv, s_send, s_recv,
):
    seq, tp, yl, core = place()
    group = seq // 4
    m = seq % 4
    z = seq // 8
    xp = group % 2
    xb = m // 2
    hy = m % 2
    hx = xb + xp - 2 * xp * xb
    cross = (1 - yl) * 2 + core
    beside = 4 * (group + 1 - 2 * xp) + (1 - xb) * 2 + hy
    root = hx * 2 + hy

    def holder(g):
        odd = g % 2
        return 4 * g + (hx + odd - 2 * odd * hx) * 2 + hy

    for d in range(4):
        greet(4 * group + d, cross)
    greet(beside, tp)

    @pl.when(z > 0)
    def _():
        greet(seq - 8, tp)

    @pl.when(z < 7)
    def _():
        greet(seq + 8, tp)

    @pl.when(group == 0)
    def _():
        @pl.loop(1, 16)
        def _(g):
            greet(holder(g), tp)

    @pl.when(group > 0)
    def _():
        greet(root, tp)

    count = 5 + jnp.where(z > 0, 1, 0) + jnp.where(z < 7, 1, 0) + jnp.where(group == 0, 15, 1)
    pl.semaphore_wait(pltpu.get_barrier_semaphore(), count)

    def piece(base, s, c):
        return pl.ds(pl.multiple_of(base + s * ROWS + c * CHUNK, 16), CHUNK)

    def head_of(d):
        b = d // 2
        return (b + xp - 2 * xp * b) * 2 + d % 2

    def spread(d, c):
        return remote(
            kv_ref.at[head_of(d), piece(0, 0, c)], kvo_ref.at[piece(OWN, m, c)],
            a_send.at[d, c], a_recv.at[m, c], 4 * group + d, cross,
        )

    def spread_q(d):
        return remote(
            q_ref.at[head_of(d)], qo_ref.at[pl.ds(pl.multiple_of(m * ROWS, 64), ROWS)],
            b_send.at[d], b_recv.at[m], 4 * group + d, cross,
        )

    for c in range(STEPS):
        for d in range(4):
            spread(d, c).start()
    for d in range(4):
        spread_q(d).start()

    def arrived(ref, sem):
        pltpu.make_async_copy(ref, ref, sem).wait()

    def across(s, c):
        return remote(
            kvo_ref.at[piece(OWN, s, c)], kvo_ref.at[piece(PREV1, s, c)],
            x_send.at[s, c], one_recv.at[s, c], beside, tp,
        )

    def passed(s, c):
        return remote(
            kvo_ref.at[piece(0, s, c)], kvo_ref.at[piece(PREV1, s, c)],
            x_send.at[s, c], one_recv.at[s, c], beside, tp,
        )

    def ahead(s, c):
        return remote(
            kvo_ref.at[piece(OWN, s, c)], kvo_ref.at[piece(0, s, c)],
            z_send.at[s, c], two_recv.at[s, c], seq + 8, tp,
        )

    def sink_copy(g):
        return remote(
            kvo_ref.at[pl.ds(OWN, 16)], kvo_ref.at[pl.ds(SINK_AT, 16)], s_send.at[g], s_recv, holder(g), tp
        )

    def needed(s, c):
        return (xp == 1) | (s > 0) | (c == STEPS - 1)

    @pl.loop(0, 20)
    def _(n):
        c = n // 4
        s = n % 4

        @pl.when(n < 16)
        def _():
            arrived(kvo_ref.at[piece(OWN, s, c)], a_recv.at[s, c])

            @pl.when(xp == 0)
            def _():
                across(s, c).start()

            @pl.when((z < 7) & needed(s, c))
            def _():
                ahead(s, c).start()

        @pl.when((n == 0) & (group == 0))
        def _():
            @pl.loop(1, 16)
            def _(g):
                sink_copy(g).start()

        @pl.when((n >= 4) & (xp == 1) & (z > 0))
        def _():
            arrived(kvo_ref.at[piece(0, s, c - 1)], two_recv.at[s, c - 1])
            passed(s, c - 1).start()

    @pl.loop(0, 16)
    def _(n):
        c = n // 4
        s = n % 4

        @pl.when((xp == 0) & (z > 0) & needed(s, c))
        def _():
            arrived(kvo_ref.at[piece(0, s, c)], two_recv.at[s, c])

        @pl.when((xp == 1) | (z > 0))
        def _():
            arrived(kvo_ref.at[piece(PREV1, s, c)], one_recv.at[s, c])

    @pl.when(group > 0)
    def _():
        arrived(kvo_ref.at[pl.ds(SINK_AT, 16)], s_recv)

    for s in range(4):
        arrived(qo_ref.at[pl.ds(s * ROWS, ROWS)], b_recv.at[s])
    for d in range(4):
        spread_q(d).wait_send()

    @pl.loop(0, 16)
    def _(n):
        c = n // 4
        s = n % 4
        spread(s, c).wait_send()

        @pl.when(xp == 0)
        def _():
            across(s, c).wait_send()

        @pl.when((xp == 1) & (z > 0))
        def _():
            passed(s, c).wait_send()

        @pl.when((z < 7) & needed(s, c))
        def _():
            ahead(s, c).wait_send()

    @pl.when(group == 0)
    def _():
        @pl.loop(1, 16)
        def _(g):
            sink_copy(g).wait_send()


def dot_t(a, b):
    return lax.dot_general(a, b, (((1,), (1,)), ((), ())), preferred_element_type=jnp.float32)


def attend_kernel(
    q_ref, kvh_ref, wo_ref, wg_ref, y_ref,
    kv, scores, o_ref, mixed, slab, padded, sem, send, recv, pass_send, lsem,
):
    seq, tp, yl, core = place()
    group = seq // 4
    m = seq % 4
    xp = group % 2
    mate = yl * 2 + 1 - core
    order = (tp, mate, (1 - yl) * 2 + core, (1 - yl) * 2 + 1 - core)
    greet(seq, mate)
    for d in range(4):
        for low in range(2):
            @pl.when((m != d) | (yl != low))
            def _():
                greet(4 * group + d, low * 2 + core)
    own_slab = pltpu.make_async_copy(wo_ref.at[:, pl.ds(pl.multiple_of(tp * PART, PART), PART)], slab, sem.at[4])
    own_slab.start()

    def load(start, size, n):
        return pltpu.make_async_copy(
            kvh_ref.at[pl.ds(start, size)], kv.at[pl.ds(start, size)], sem.at[n]
        )

    def blank(start, size):
        mark = lax.broadcasted_iota(jnp.int32, (16, 2 * PAD), 1)
        row = jnp.where(mark == 102, 1.0, 0.0).astype(jnp.bfloat16)

        @pl.loop(0, size // 16)
        def _(n):
            kv[pl.ds(pl.multiple_of(start + n * 16, 16), 16), :] = row

    pieces = ((OWN, GROUP, 0), (PREV1, GROUP, 1), (FAR, GROUP - FAR, 2), (SINK_AT, 16, 1))
    for n, (start, size, least) in enumerate(pieces):
        @pl.when(group >= least)
        def _():
            load(start, size, n).start()

        @pl.when(group < least)
        def _():
            blank(start, size)

    for n in range(16):
        padded[pl.ds(n * PAD + HD, PAD - HD), :] = jnp.zeros((PAD - HD, PART), jnp.bfloat16)
    for n in range(12):
        padded[pl.ds((n + 4) * PAD, HD), :] = wg_ref[n // 4, pl.ds(n % 4 * HD, HD), :]
    own_slab.wait()
    for n in range(4):
        padded[pl.ds(n * PAD, HD), :] = slab[pl.ds(n * HD, HD), :]
    for n, (start, size, least) in enumerate(pieces):
        @pl.when(group >= least)
        def _():
            load(start, size, n).wait()

    pl.semaphore_wait(pltpu.get_barrier_semaphore(), 8)

    def key(start, size):
        return kv[pl.ds(pl.multiple_of(start, TILE), size), 0:PAD]

    def val(start, size):
        return kv[pl.ds(pl.multiple_of(start, TILE), size), PAD:]

    down = lax.broadcasted_iota(jnp.int32, (TILE, TILE), 0)
    right = lax.broadcasted_iota(jnp.int32, (TILE, TILE), 1)
    lower = right <= down
    sink_k = kv[pl.ds(SINK_AT, 16), 0:PAD]
    sink_v = kv[pl.ds(SINK_AT, 16), PAD:]
    small_down = lax.broadcasted_iota(jnp.int32, (TILE, 16), 0)
    small_right = lax.broadcasted_iota(jnp.int32, (TILE, 16), 1)

    def finish(rows, acc):
        lane = lanes(TILE)
        out = acc * (1.0 / acc[:, HD:HD + 1])
        o_ref[rows, :] = jnp.where(lane < HD, out, 0.0).astype(jnp.bfloat16)

    def long_tile(i, rows, first):
        q = q_ref[rows, :]
        near = OWN + i * TILE
        outer = FAR + i * TILE
        s = jnp.where(lower, dot_t(q, key(near, TILE)), dot_t(q, key(outer, TILE)))
        scores[:, 0:TILE] = s
        top = jnp.maximum(s[:, :PAD], s[:, PAD:])
        distance = first + small_down - small_right
        seen = (small_right < SINKS) & (distance >= WINDOW)
        sink_s = jnp.where(seen, dot_t(q, sink_k), NEG)
        for c in range(5):
            s = dot_t(q, key(outer + TILE + c * 768, 768))
            scores[:, pl.ds(TILE + c * 768, 768)] = s
            for n in range(6):
                top = jnp.maximum(top, s[:, n * PAD:(n + 1) * PAD])
        peak = jnp.maximum(
            jnp.max(top, axis=-1, keepdims=True), jnp.max(sink_s, axis=-1, keepdims=True)
        )
        w = jnp.where(seen, jnp.exp2(sink_s - peak), 0.0).astype(jnp.bfloat16)
        acc = jnp.dot(w, sink_v, preferred_element_type=jnp.float32)
        w = jnp.exp2(scores[:, 0:TILE] - peak)
        acc += jnp.dot(
            jnp.where(lower, w, 0.0).astype(jnp.bfloat16), val(near, TILE), preferred_element_type=jnp.float32
        )
        acc += jnp.dot(
            jnp.where(lower, 0.0, w).astype(jnp.bfloat16), val(outer, TILE), preferred_element_type=jnp.float32
        )
        for c in range(5):
            w = jnp.exp2(scores[:, pl.ds(TILE + c * 768, 768)] - peak).astype(jnp.bfloat16)
            acc += jnp.dot(w, val(outer + TILE + c * 768, 768), preferred_element_type=jnp.float32)
        finish(rows, acc)

    def mixed_tile(i, rows, first):
        q = q_ref[rows, :]
        lane = lanes(TILE)
        qf = q.astype(jnp.float32)
        mine = qf[:, 101:102]
        pick = jnp.where(lane == 96, -1.0, jnp.where(lane == 97, mine, 0.0)).astype(jnp.bfloat16)
        lost = jnp.where(lane == 100, 1.0, 0.0).astype(jnp.bfloat16)
        distance = first + small_down - small_right
        seen = (small_right < SINKS) & (distance >= WINDOW) & (dot_t(pick, sink_k) == 0.0)
        sink_s = jnp.where(seen, dot_t(q, sink_k), NEG)
        peak = jnp.max(sink_s, axis=-1, keepdims=True)
        w = jnp.where(seen, jnp.exp2(sink_s - peak), 0.0).astype(jnp.bfloat16)
        acc = jnp.dot(w, sink_v, preferred_element_type=jnp.float32)
        low = jnp.where(first >= LONG, 15, 0)

        def step(n, carry):
            peak, acc = carry
            start = FAR + i * TILE + n * TILE
            k = key(start, TILE)
            gap = (16 - n) * TILE + down - right
            bad = dot_t(lost, k)
            seen = (gap >= 0) & (gap < WINDOW) & (dot_t(pick, k) == 0.0) & ((bad < 0.5) | (gap == 0))
            s = jnp.where(seen, dot_t(q, k), NEG)
            now = jnp.maximum(peak, jnp.max(s, axis=-1, keepdims=True))
            w = jnp.where(seen, jnp.exp2(s - now), 0.0).astype(jnp.bfloat16)
            acc = acc * jnp.exp2(peak - now) + jnp.dot(w, val(start, TILE), preferred_element_type=jnp.float32)
            return now, acc

        peak, acc = lax.fori_loop(low, 17, step, (peak, acc))
        finish(rows, acc)

    def head(member, low, who):
        b = member // 2
        return 4 * ((1 - low) * 2 + who) + (b + xp - 2 * xp * b) * 2 + member % 2

    mine = head(m, yl, core)
    halves = (pl.ds(0, 320), pl.ds(320, 256))

    def out(d, half, low):
        source = pl.ds(pl.multiple_of(d * ROWS + half * 320, 64), 256 if half else 320)
        return remote(
            o_ref.at[source], mixed.at[mine, halves[half]],
            send.at[d, half, low], recv.at[mine, half], 4 * group + d, low * 2 + core,
        )

    def local(d, half):
        source = pl.ds(pl.multiple_of(d * ROWS + half * 320, 64), 256 if half else 320)
        return pltpu.make_async_copy(o_ref.at[source], mixed.at[mine, halves[half]], lsem.at[half])

    def onward(d, half, low):
        g = head(d, low, core)
        ref = mixed.at[g, halves[half]]
        return remote(ref, ref, pass_send.at[d, half, low], recv.at[g, half], seq, mate)

    def arrived(g, half):
        ref = mixed.at[g, halves[half]]
        pltpu.make_async_copy(ref, ref, recv.at[g, half]).wait()

    def give(d, half):
        for low in range(2):
            @pl.when((m != d) | (yl != low))
            def _():
                out(d, half, low).start()

            @pl.when((m == d) & (yl == low))
            def _():
                local(d, half).start()

    def relay(half):
        for d in range(4):
            for low in range(2):
                @pl.when((m != d) | (yl != low))
                def _():
                    arrived(head(d, low, core), half)

                @pl.when((m == d) & (yl == low))
                def _():
                    local(d, half).wait()

                onward(d, half, low).start()

    tiles = GROUP // TILE

    @pl.loop(0, tiles + 1)
    def _(i):
        rows = pl.ds(pl.multiple_of(jnp.minimum(i, tiles - 1) * TILE, TILE), TILE)
        first = group * GROUP + i * TILE

        @pl.when((i < tiles) & (first + TILE <= LONG))
        def _():
            long_tile(i, rows, first)

        @pl.when((i < tiles) & (first + TILE > LONG))
        def _():
            mixed_tile(i, rows, first)

        for half in range(2):
            @pl.when((i > 0) & (i < tiles) & ((i + 1) % 2 == half))
            def _():
                give((i - 1) // 2, half)

            @pl.when((i > 1) & (i - 2 == 2 * m + half))
            def _():
                relay(half)

    partner = 1 - core
    for half in range(2):
        for d in range(4):
            for low in range(2):
                arrived(head(d, low, partner), half)
        size = 160 - 32 * half
        for n in range(2):
            rows = pl.ds(half * 320 + n * size, size)
            left = jnp.concatenate(
                [mixed[4 * order[k // 4] + k % 4, rows, :] for k in range(16)], axis=1
            )
            y_ref[rows, :] = jnp.dot(
                left, padded[...], preferred_element_type=jnp.float32
            ).astype(jnp.bfloat16)
    for d in range(4):
        for half in range(2):
            for low in range(2):
                @pl.when((m != d) | (yl != low))
                def _():
                    out(d, half, low).wait_send()

                onward(d, half, low).wait_send()


def shards(tokens, norm_gain, w_qkv, w_out, sink_logit, segment_ids, positions, padding_mask):
    bf16, f32 = jnp.bfloat16, jnp.float32
    spot = jnp.arange(PAD, dtype=jnp.int32)
    freq = THETA ** (-((spot % 48).astype(f32) * 2.0 / HD))
    angle = positions.astype(f32)[:, None] * freq[None, :]
    cosine = jnp.cos(angle)
    sine = jnp.where(spot[None, :] < 48, -jnp.sin(angle), jnp.sin(angle))
    seg = segment_ids.astype(f32)[:, None]
    sinkish = (positions < SINKS).astype(f32)[:, None]
    lost = 1.0 - padding_mask.astype(f32)[:, None]
    kmark = jnp.where(spot == 96, seg, 0.0) + jnp.where(spot == 97, 1.0, 0.0)
    kmark = kmark + jnp.where((spot == 98) | (spot == 99), sinkish, 0.0) + jnp.where(spot == 100, lost, 0.0)
    qmark = jnp.where(spot == 101, seg, 0.0) + jnp.where(spot == 102, NEG, 0.0)
    logit = sink_logit * (1.0 / math.log(2.0))
    high = lax.reduce_precision(logit, 8, 7)
    low = logit - high
    sink = jnp.where(spot == 98, high[:, None], 0.0) + jnp.where(spot == 99, low[:, None], 0.0)
    sink = sink.reshape(4, 1, PAD)

    dma = pltpu.SemaphoreType.DMA
    q, kv, cache, wg = pl.pallas_call(
        project_kernel,
        out_shape=(
            jax.ShapeDtypeStruct((4, ROWS, PAD), bf16),
            jax.ShapeDtypeStruct((4, ROWS, 2 * PAD), bf16),
            jax.ShapeDtypeStruct((2, ROWS, WIDTH), bf16),
            jax.ShapeDtypeStruct((3, WIDTH, PART), bf16),
        ),
        in_specs=[ANY, VM, ANY, VM, VM, VM, VM, VM, ANY],
        out_specs=(VM, VM, VM, ANY),
        scratch_shapes=[
            pltpu.VMEM((4, ROWS, PART), bf16),
            pltpu.VMEM((4, 3, PART, WIDTH), bf16),
            pltpu.VMEM((ROWS, 3 * WIDTH), f32),
            pltpu.VMEM((ROWS, 1), f32),
            dma((4,)),
            dma,
            dma((9,)),
            dma((9,)),
            dma((3,)),
            dma((3,)),
        ],
        compiler_params=pltpu.CompilerParams(collective_id=0, has_side_effects=True),
        name="project",
    )(
        tokens, norm_gain.reshape(4, 1, PART), jnp.transpose(w_qkv, (1, 0, 2)),
        cosine, sine, kmark, qmark, sink, w_out,
    )
    qo, kvo = pl.pallas_call(
        exchange_kernel,
        out_shape=(
            jax.ShapeDtypeStruct((GROUP, PAD), bf16),
            jax.ShapeDtypeStruct((SPAN, 2 * PAD), bf16),
        ),
        in_specs=[ANY, ANY],
        out_specs=(ANY, ANY),
        scratch_shapes=[
            dma((4, 4)), dma((4, 4)), dma((4,)), dma((4,)), dma((4, 4)), dma((4, 4)),
            dma((4, 4)), dma((4, 4)), dma((16,)), dma,
        ],
        compiler_params=pltpu.CompilerParams(collective_id=1, has_side_effects=True),
        name="exchange",
    )(q, kv)
    y = pl.pallas_call(
        attend_kernel,
        out_shape=jax.ShapeDtypeStruct((ROWS, PART), bf16),
        in_specs=[VM, ANY, ANY, VM],
        out_specs=VM,
        scratch_shapes=[
            pltpu.VMEM((SPAN, 2 * PAD), bf16),
            pltpu.VMEM((TILE, WINDOW), f32),
            pltpu.VMEM((GROUP, PAD), bf16),
            pltpu.VMEM((16, ROWS, PAD), bf16),
            pltpu.VMEM((WIDTH, PART), bf16),
            pltpu.VMEM((16 * PAD, PART), bf16),
            dma((5,)),
            dma((4, 2, 2)),
            dma((16, 2)),
            dma((4, 2, 2)),
            dma((2,)),
        ],
        compiler_params=pltpu.CompilerParams(collective_id=2, has_side_effects=True),
        name="attend",
    )(qo, kvo, w_out, wg)
    return (y, cache)


def solution(mesh):
    return jax.shard_map(
        shards,
        mesh=mesh,
        in_specs=(
            P("seq", "tp"),
            P(),
            P(None, None, "tp"),
            P("tp", None),
            P("tp"),
            P("seq"),
            P("seq"),
            P("seq"),
        ),
        out_specs=(P("seq", "tp"), P(None, "seq", "tp")),
        check_vma=False,
    )
```

time: 154 us -> 143 us (0.929)
  the two profiles are of different devices: /device:TPU:241 before, /device:TPU:243 now
where the time goes in v2:
time: 143 us
  Pallas kernels  132 us (92%)
  other arithmetic  7.13 us (5%)
  local copies, waits for them, and re-layouts  3.13 us (2%)
    pallas_call x1, Pallas kernels, shards(): pl.pallas_call(attend_kernel, out_shape=jax.ShapeDtypeStruct((ROWS, PART)...  62.6 us
    pallas_call x1, Pallas kernels, shards(): pl.pallas_call(exchange_kernel, out_shape=(jax.ShapeDtypeStruct((GROUP, P...  37.5 us
    pallas_call x1, Pallas kernels, shards(): pl.pallas_call(project_kernel, out_shape=(jax.ShapeDtypeStruct((4, ROWS,...  31.6 us
    unnamed x4, local copies, waits for them, and re-layouts  3.13 us

profile of v2, /device:TPU:243, one launch (start us, length us, event | category | flops | bytes accessed | tf_op | source)
XLA Modules:
  0.0 142.6 jit_solution(4736194663823094936)
XLA Ops:
  0.7 0.7 multiply_reduce-precision_fusion
  1.3 0.7 fusion.sink_ref
  2.0 0.7 convert_element_type.21
  2.7 0.7 convert_subtract_fusion
  3.4 0.7 compare_convert_fusion
  4.1 0.7 convert_element_type.19
  4.8 1.1 select_add_fusion
  5.8 1.9 %negate_select_fusion = (f32[576,128]{1,0:T(8,128)}, f32[576,128]{1,0:T(8,128)}) fusion(f32[128]{0:T(128)S(1)} %fusion.4, f32[576]{0:T(1024)S(1)} %convert_element_type.19, pred[128]{0:T(512)(128)(4,1)S(1)} %iota_compare_fusion.5), kind=kLoop, calls=%fused_computation | loop fusion | flops 221184 | bytes 592768 | tf_op jit(solution)/shard_map/jit(_where)/select_n | solution.py:645
  7.8 31.6 %project.1 = (bf16[4,576,128]{2,1,0:T(8,128)(2,1)}, bf16[4,576,256]{2,1,0:T(8,128)(2,1)}, bf16[2,576,384]{2,1,0:T(8,128)(2,1)}, bf16[3,384,768]{2,1,0:T(8,128)(2,1)}) custom-call(bf16[576,768]{1,0:T(8,128)(2,1)} %x_ref.1, f32[4,1,768]{2,1,0:T(1,128)} %bitcast.3, bf16[3,3072,384]{2,1,0:T(8,128)(2,1)} %bitcast.2, f32[576,128]{1,0:T(8,128)} %get-tuple-element.15.cos_ref, ...), custom_call_target="tpu_custom_call" | custom-call | tf_op jit(solution)/shard_map/project/pallas_call | solution.py:659
  39.3 37.5 %exchange.1 = (bf16[2304,128]{1,0:T(8,128)(2,1)}, bf16[6928,256]{1,0:T(8,128)(2,1)}) custom-call(bf16[4,576,128]{2,1,0:T(8,128)(2,1)} %get-tuple-element.8.q_ref, bf16[4,576,256]{2,1,0:T(8,128)(2,1)} %get-tuple-element.9.kv_ref), custom_call_target="tpu_custom_call" | custom-call | tf_op jit(solution)/shard_map/exchange/pallas_call | solution.py:687
  76.9 62.6 %attend.1 = bf16[576,768]{1,0:T(8,128)(2,1)} custom-call(bf16[2304,128]{1,0:T(8,128)(2,1)} %get-tuple-element.10.q_ref, bf16[6928,256]{1,0:T(8,128)(2,1)} %get-tuple-element.11.kvh_ref, bf16[384,3072]{1,0:T(8,128)(2,1)} %wo_ref.3, bf16[3,384,768]{2,1,0:T(8,128)(2,1)} %get-tuple-element.12.wg_ref), custom_call_target="tpu_custom_call" | custom-call | tf_op jit(solution)/shard_map/attend/pallas_call | solution.py:702
  139.5 0.0 copy-start
  139.5 2.2 %copy.12 = bf16[576,768]{1,0:T(8,128)(2,1)} copy(bf16[576,768]{1,0:T(8,128)(2,1)} %attend.1) | data formatting | bytes 1769472
  141.7 0.0 copy-done
  141.7 0.9 copy.13
  (6 shorter events, 0.0 us)
Async XLA Ops:
  139.5 2.2 %copy-start = (bf16[2,576,384]{2,1,0:T(8,128)(2,1)S(1)}, bf16[2,576,384]{2,1,0:T(8,128)(2,1)}, u32[]{:S(2)}) copy-start(bf16[2,576,384]{2,1,0:T(8,128)(2,1)} %get-tuple-element.31) | copy-start | bytes 2654212

commit v3 on v2

v3 whole, which is shorter than its diff:
```python
import math

import jax
import jax.numpy as jnp
import numpy as np
from jax import lax
from jax.experimental import pallas as pl
from jax.experimental.pallas import tpu as pltpu
from jax.sharding import PartitionSpec as P

WINDOW = 4096
SINKS = 4
EPS = 1e-05
THETA = 10000.0
LONG = 32832

ROWS = 576
MODEL = 3072
PART = 768
WIDTH = 384
HD = 96
PAD = 128
GROUP = 2304
TILE = 256
CHUNK = 144
STEPS = 4
PREV1 = GROUP
OWN = 2 * GROUP
SINK_AT = 3 * GROUP
SPAN = 3 * GROUP + 16
FAR = 512
NEG = -1e30
MESH = pl.DeviceIdType.MESH
ANY = pl.BlockSpec(memory_space=pl.ANY)
VM = pl.BlockSpec(memory_space=pltpu.VMEM)


def place():
    seq = lax.axis_index("seq")
    tp = lax.axis_index("tp")
    return seq, tp, tp // 2, tp % 2


def remote(src, dst, send, recv, seq, tp):
    return pltpu.make_async_remote_copy(
        src_ref=src,
        dst_ref=dst,
        send_sem=send,
        recv_sem=recv,
        device_id=(seq, tp),
        device_id_type=MESH,
    )


def arrived(ref, sem):
    pltpu.make_async_copy(ref, ref, sem).wait()


def greet(seq, tp):
    pl.semaphore_signal(
        pltpu.get_barrier_semaphore(), inc=1, device_id=(seq, tp), device_id_type=MESH
    )


def lanes(rows):
    return lax.broadcasted_iota(jnp.int32, (rows, PAD), 1)


def dot_t(a, b):
    return lax.dot_general(a, b, (((1,), (1,)), ((), ())), preferred_element_type=jnp.float32)


def whole_kernel(
    x_ref, gain_ref, w_ref, info_ref, freq_ref, logit_ref, wo_ref,
    y_ref, cache_ref,
    held, weights, acc, square, mark_s, q_s, kv_s, qo, kv, scores, o_ref, mixed, wg, slab, padded,
    wsem, xsem, send, recv, wsend, wrecv, a_send, a_recv, b_send, b_recv,
    x_send, z_send, one_recv, two_recv, s_send, s_recv, o_send, o_recv, pass_send, lsem,
):
    seq, tp, yl, core = place()
    group = seq // 4
    m = seq % 4
    z = seq // 8
    xp = group % 2
    xb = m // 2
    hy = m % 2
    mate = yl * 2 + 1 - core
    cross = (1 - yl) * 2 + core
    far = (1 - yl) * 2 + 1 - core
    flipped = seq + 1 - 2 * hy
    beside = 4 * (group + 1 - 2 * xp) + (1 - xb) * 2 + hy
    order = (tp, mate, cross, far)

    def wide(t):
        return pl.ds(pl.multiple_of(t * PART, PART), PART)

    own = pltpu.make_async_copy(x_ref, held.at[0], xsem)
    own.start()

    def weight_copy(k):
        return pltpu.make_async_copy(w_ref.at[:, wide(order[k]), :], weights.at[k], wsem.at[k])

    for k in range(4):
        weight_copy(k).start()
    own_slab = pltpu.make_async_copy(wo_ref.at[:, wide(tp)], slab, wsem.at[4])
    own_slab.start()

    greet(seq, mate)
    greet(flipped, far)
    greet(beside, tp)
    for d in range(4):
        for low in range(2):
            @pl.when((m != d) | (yl != low))
            def _():
                greet(4 * group + d, low * 2 + core)

    @pl.when(z > 0)
    def _():
        greet(seq - 8, tp)

    @pl.when(z < 7)
    def _():
        greet(seq + 8, tp)

    pl.semaphore_wait(
        pltpu.get_barrier_semaphore(), 10 + jnp.where(z > 0, 1, 0) + jnp.where(z < 7, 1, 0)
    )

    def part(c):
        return pl.ds(pl.multiple_of(c * CHUNK, CHUNK), CHUNK)

    def to_cross(c):
        return remote(x_ref.at[part(c)], held.at[2, part(c)], send.at[c], recv.at[c], seq, cross)

    def onward_x(c):
        return remote(
            held.at[2, part(c)], held.at[3, part(c)], send.at[4 + c], recv.at[4 + c], seq, mate
        )

    @pl.loop(0, STEPS)
    def _(c):
        to_cross(c).start()

    to_mate = remote(x_ref, held.at[1], send.at[8], recv.at[8], seq, mate)
    to_mate.start()
    slabs = [
        remote(wo_ref.at[:, wide(t2)], wg.at[n], wsend.at[n], wrecv.at[n], s2, t2)
        for n, (s2, t2) in enumerate(((seq, mate), (flipped, cross), (flipped, far)))
    ]
    for copy in slabs:
        copy.start()

    def blank(start, size):
        mark = lax.broadcasted_iota(jnp.int32, (16, 2 * PAD), 1)
        row = jnp.where(mark == 102, 1.0, 0.0).astype(jnp.bfloat16)

        @pl.loop(0, size // 16)
        def _(n):
            kv[pl.ds(pl.multiple_of(start + n * 16, 16), 16), :] = row

    @pl.when(group == 0)
    def _():
        blank(PREV1, GROUP)
        blank(SINK_AT, 16)

    @pl.when(group < 2)
    def _():
        blank(FAR, GROUP - FAR)

    lane_row = lanes(1)
    sinks = []
    for h in range(4):
        logit = jnp.full((1, PAD), logit_ref[h], jnp.float32) * (1.0 / math.log(2.0))
        high = logit.astype(jnp.bfloat16).astype(jnp.float32)
        sinks.append(jnp.where(lane_row == 98, high, jnp.where(lane_row == 99, logit - high, 0.0)))

    def tables(c):
        rows = part(c)
        lane = lanes(CHUNK)
        info = info_ref[rows, :]
        pos = info[:, 0:1]
        seg = info[:, 1:2]
        lost = 1.0 - info[:, 2:3]
        first = jnp.where(pos < SINKS, 1.0, 0.0)
        mark_s[0, rows, :] = jnp.where(
            lane == 96, seg,
            jnp.where(
                lane == 97, 1.0,
                jnp.where((lane == 98) | (lane == 99), first, jnp.where(lane == 100, lost, 0.0)),
            ),
        )
        mark_s[1, rows, :] = jnp.where(lane == 101, seg, jnp.where(lane == 102, NEG, 0.0))
        turns = pos * freq_ref[0:1, :]
        turns = (turns - jnp.round(turns)) + pos * freq_ref[1:2, :]
        angle = (turns - jnp.round(turns)) * (2.0 * math.pi)
        sine = jnp.sin(angle)
        mark_s[2, rows, :] = jnp.cos(angle)
        mark_s[3, rows, :] = jnp.where(lane < 48, -sine, sine)

    def block(k, c):
        rows = part(c)
        x = held[k, rows, :].astype(jnp.float32)
        sums = jnp.sum(x * x, axis=-1, keepdims=True)
        y = (x * gain_ref[:, wide(order[k])]).astype(jnp.bfloat16)
        if k == 0:
            square[rows, :] = sums
        else:
            square[rows, :] += sums
        for j in range(3):
            cols = pl.ds(j * WIDTH, WIDTH)
            term = jnp.dot(y, weights[k, j], preferred_element_type=jnp.float32)
            if k == 0:
                acc[rows, cols] = term
            else:
                acc[rows, cols] += term

    def close(c):
        rows = part(c)
        lane = lanes(CHUNK)
        factor = lax.rsqrt(square[rows, :] / MODEL + EPS)
        info = info_ref[rows, :]
        valid = info[:, 2:3]
        kmark = mark_s[0, rows, :]
        qmark = mark_s[1, rows, :]
        cosine = mark_s[2, rows, :]
        sine = mark_s[3, rows, :]

        def heads(j):
            b = [acc[rows, pl.ds(j * WIDTH + n * PAD, PAD)] * factor for n in range(3)]
            return b, [
                b[0],
                jnp.where(lane < 32, pltpu.roll(b[0], 32, 1), pltpu.roll(b[1], 32, 1)),
                jnp.where(lane < 64, pltpu.roll(b[1], 64, 1), pltpu.roll(b[2], 64, 1)),
                pltpu.roll(b[2], 96, 1),
            ]

        def turn(u):
            other = jnp.where(lane < 48, pltpu.roll(u, 80, 1), pltpu.roll(u, 48, 1))
            return jnp.where(lane < HD, u * cosine + other * sine, 0.0)

        for h, u in enumerate(heads(0)[1]):
            full = turn(u) * (HD ** -0.5 / math.log(2.0)) + qmark + sinks[h]
            q_s[h, rows, :] = full.astype(jnp.bfloat16)
        keys = []
        for h, u in enumerate(heads(1)[1]):
            k = turn(u)
            keys.append(k)
            kv_s[h, rows, 0:PAD] = (k + kmark).astype(jnp.bfloat16)
        k1, k2, k3 = (pltpu.roll(keys[1], 96, 1), pltpu.roll(keys[2], 64, 1), pltpu.roll(keys[3], 32, 1))
        joined = (
            jnp.where(lane < 96, keys[0], k1),
            jnp.where(lane < 64, k1, k2),
            jnp.where(lane < 32, k2, k3),
        )
        plain, values = heads(2)
        for n in range(3):
            cols = pl.ds(n * PAD, PAD)
            cache_ref[0, rows, cols] = (joined[n] * valid).astype(jnp.bfloat16)
            cache_ref[1, rows, cols] = (plain[n] * valid).astype(jnp.bfloat16)
        for h, u in enumerate(values):
            v = jnp.where(lane < HD, u, jnp.where(lane == HD, 1.0, 0.0))
            kv_s[h, rows, PAD:] = v.astype(jnp.bfloat16)

    def piece(base, s, c):
        return pl.ds(pl.multiple_of(base + s * ROWS + c * CHUNK, 16), CHUNK)

    def head_of(d):
        b = d // 2
        return (b + xp - 2 * xp * b) * 2 + d % 2

    def spread(d, c):
        return remote(
            kv_s.at[head_of(d), part(c)], kv.at[piece(OWN, m, c)],
            a_send.at[d, c], a_recv.at[m, c], 4 * group + d, cross,
        )

    def spread_q(d, c):
        return remote(
            q_s.at[head_of(d), part(c)], qo.at[piece(0, m, c)],
            b_send.at[d, c], b_recv.at[m, c], 4 * group + d, cross,
        )

    def across(s, c):
        return remote(
            kv.at[piece(OWN, s, c)], kv.at[piece(PREV1, s, c)],
            x_send.at[s, c], one_recv.at[s, c], beside, tp,
        )

    def passed(s, c):
        return remote(
            kv.at[piece(0, s, c)], kv.at[piece(PREV1, s, c)],
            x_send.at[s, c], one_recv.at[s, c], beside, tp,
        )

    def ahead(s, c):
        return remote(
            kv.at[piece(OWN, s, c)], kv.at[piece(0, s, c)],
            z_send.at[s, c], two_recv.at[s, c], seq + 8, tp,
        )

    sink_rows = kv.at[pl.ds(SINK_AT, 16)]
    sink_from = kv.at[pl.ds(pl.multiple_of(jnp.where(z == 0, OWN, SINK_AT), 16), 16)]
    sink_beside = remote(sink_from, sink_rows, s_send.at[0], s_recv, beside, tp)
    sink_ahead = remote(sink_from, sink_rows, s_send.at[1], s_recv, seq + 8, tp)

    def needed(s, c):
        return (xp == 1) | (s > 0) | (c == STEPS - 1)

    def serve(n):
        c = n // 4
        s = n % 4

        @pl.when(n < 16)
        def _():
            arrived(kv.at[piece(OWN, s, c)], a_recv.at[s, c])

            @pl.when(xp == 0)
            def _():
                across(s, c).start()

            @pl.when((z < 7) & needed(s, c))
            def _():
                ahead(s, c).start()

        @pl.when((n == z) & (xp == 0))
        def _():
            @pl.when(z > 0)
            def _():
                arrived(sink_rows, s_recv)

            sink_beside.start()

            @pl.when(z < 7)
            def _():
                sink_ahead.start()

        @pl.when((n >= 4) & (xp == 1) & (z > 0))
        def _():
            arrived(kv.at[piece(0, s, c - 1)], two_recv.at[s, c - 1])
            passed(s, c - 1).start()

    @pl.loop(0, STEPS)
    def _(c):
        tables(c)

    own.wait()
    weight_copy(0).wait()

    @pl.loop(0, STEPS)
    def _(c):
        block(0, c)

    to_mate.wait_recv()
    weight_copy(1).wait()

    @pl.loop(0, STEPS)
    def _(c):
        block(1, c)

    weight_copy(2).wait()
    weight_copy(3).wait()

    @pl.loop(0, STEPS + 1)
    def _(c):
        @pl.when(c < STEPS)
        def _():
            to_cross(c).wait_recv()
            onward_x(c).start()
            block(2, c)

        @pl.when(c > 0)
        def _():
            onward_x(c - 1).wait_recv()
            block(3, c - 1)
            close(c - 1)
            for d in range(4):
                spread(d, c - 1).start()
            for d in range(4):
                spread_q(d, c - 1).start()

        @pl.when(c > 2)
        def _():
            @pl.loop(0, 4)
            def _(n):
                serve((c - 3) * 4 + n)

    @pl.loop(8, 20)
    def _(n):
        serve(n)

    for copy in slabs:
        copy.wait_recv()
    own_slab.wait()
    for n in range(16):
        padded[pl.ds(n * PAD + HD, PAD - HD), :] = jnp.zeros((PAD - HD, PART), jnp.bfloat16)
    for n in range(12):
        padded[pl.ds((n + 4) * PAD, HD), :] = wg[n // 4, pl.ds(n % 4 * HD, HD), :]
    for n in range(4):
        padded[pl.ds(n * PAD, HD), :] = slab[pl.ds(n * HD, HD), :]

    @pl.loop(0, 16)
    def _(n):
        c = n // 4
        s = n % 4
        arrived(qo.at[piece(0, s, c)], b_recv.at[s, c])

        @pl.when((xp == 0) & (z > 0) & needed(s, c))
        def _():
            arrived(kv.at[piece(0, s, c)], two_recv.at[s, c])

        @pl.when((xp == 1) | (z > 0))
        def _():
            arrived(kv.at[piece(PREV1, s, c)], one_recv.at[s, c])

    @pl.when(xp == 1)
    def _():
        arrived(sink_rows, s_recv)

    def key(start, size):
        return kv[pl.ds(pl.multiple_of(start, TILE), size), 0:PAD]

    def val(start, size):
        return kv[pl.ds(pl.multiple_of(start, TILE), size), PAD:]

    down = lax.broadcasted_iota(jnp.int32, (TILE, TILE), 0)
    right = lax.broadcasted_iota(jnp.int32, (TILE, TILE), 1)
    lower = right <= down
    sink_k = kv[pl.ds(SINK_AT, 16), 0:PAD]
    sink_v = kv[pl.ds(SINK_AT, 16), PAD:]
    small_down = lax.broadcasted_iota(jnp.int32, (TILE, 16), 0)
    small_right = lax.broadcasted_iota(jnp.int32, (TILE, 16), 1)

    def finish(rows, acc):
        lane = lanes(TILE)
        out = acc * (1.0 / acc[:, HD:HD + 1])
        o_ref[rows, :] = jnp.where(lane < HD, out, 0.0).astype(jnp.bfloat16)

    def long_tile(i, rows, first):
        q = qo[rows, :]
        near = OWN + i * TILE
        outer = FAR + i * TILE
        s = jnp.where(lower, dot_t(q, key(near, TILE)), dot_t(q, key(outer, TILE)))
        scores[:, 0:TILE] = s
        top = jnp.maximum(s[:, :PAD], s[:, PAD:])
        distance = first + small_down - small_right
        seen = (small_right < SINKS) & (distance >= WINDOW)
        sink_s = jnp.where(seen, dot_t(q, sink_k), NEG)
        for c in range(5):
            s = dot_t(q, key(outer + TILE + c * 768, 768))
            scores[:, pl.ds(TILE + c * 768, 768)] = s
            for n in range(6):
                top = jnp.maximum(top, s[:, n * PAD:(n + 1) * PAD])
        peak = jnp.maximum(
            jnp.max(top, axis=-1, keepdims=True), jnp.max(sink_s, axis=-1, keepdims=True)
        )
        w = jnp.where(seen, jnp.exp2(sink_s - peak), 0.0).astype(jnp.bfloat16)
        acc = jnp.dot(w, sink_v, preferred_element_type=jnp.float32)
        w = jnp.exp2(scores[:, 0:TILE] - peak)
        acc += jnp.dot(
            jnp.where(lower, w, 0.0).astype(jnp.bfloat16), val(near, TILE), preferred_element_type=jnp.float32
        )
        acc += jnp.dot(
            jnp.where(lower, 0.0, w).astype(jnp.bfloat16), val(outer, TILE), preferred_element_type=jnp.float32
        )
        for c in range(5):
            w = jnp.exp2(scores[:, pl.ds(TILE + c * 768, 768)] - peak).astype(jnp.bfloat16)
            acc += jnp.dot(w, val(outer + TILE + c * 768, 768), preferred_element_type=jnp.float32)
        finish(rows, acc)

    def mixed_tile(i, rows, first):
        q = qo[rows, :]
        lane = lanes(TILE)
        qf = q.astype(jnp.float32)
        mine = qf[:, 101:102]
        pick = jnp.where(lane == 96, -1.0, jnp.where(lane == 97, mine, 0.0)).astype(jnp.bfloat16)
        lost = jnp.where(lane == 100, 1.0, 0.0).astype(jnp.bfloat16)
        distance = first + small_down - small_right
        seen = (small_right < SINKS) & (distance >= WINDOW) & (dot_t(pick, sink_k) == 0.0)
        sink_s = jnp.where(seen, dot_t(q, sink_k), NEG)
        peak = jnp.max(sink_s, axis=-1, keepdims=True)
        w = jnp.where(seen, jnp.exp2(sink_s - peak), 0.0).astype(jnp.bfloat16)
        acc = jnp.dot(w, sink_v, preferred_element_type=jnp.float32)
        low = jnp.where(first >= LONG, 15, 0)

        def step(n, carry):
            peak, acc = carry
            start = FAR + i * TILE + n * TILE
            k = key(start, TILE)
            gap = (16 - n) * TILE + down - right
            bad = dot_t(lost, k)
            seen = (gap >= 0) & (gap < WINDOW) & (dot_t(pick, k) == 0.0) & ((bad < 0.5) | (gap == 0))
            s = jnp.where(seen, dot_t(q, k), NEG)
            now = jnp.maximum(peak, jnp.max(s, axis=-1, keepdims=True))
            w = jnp.where(seen, jnp.exp2(s - now), 0.0).astype(jnp.bfloat16)
            acc = acc * jnp.exp2(peak - now) + jnp.dot(w, val(start, TILE), preferred_element_type=jnp.float32)
            return now, acc

        peak, acc = lax.fori_loop(low, 17, step, (peak, acc))
        finish(rows, acc)

    def head(member, low, who):
        b = member // 2
        return 4 * ((1 - low) * 2 + who) + (b + xp - 2 * xp * b) * 2 + member % 2

    mine = head(m, yl, core)
    outer = (m == 0) | (m == 3)
    begins = ((0, 192, 128, 320), (256, 0, 384, 64), (512, 448, 0, 0))
    turn_of = ((0, 2, 3, 1), (4, 6, 7, 5))
    parcels = (
        ((0, 0),), ((0, 1),), ((0, 2), (1, 1)), ((1, 0),), ((1, 2), (2, 2)),
        ((2, 0),), ((2, 1), (3, 2)), ((3, 1),), ((3, 0),),
    )
    sequence = (0, 8, 3, 5, 1, 7, 2, 6, 4)

    def size_of(d, p):
        return (256, 256, 64)[p] if d in (0, 3) else (256, 192, 128)[p]

    def pick_of(table, k):
        return jnp.where(k == 0, table[0], jnp.where(k == 1, table[1], jnp.where(k == 2, table[2], table[3])))

    def my_rows(p, size):
        return pl.ds(pl.multiple_of(pick_of(begins[p], m), 64), size)

    def out(d, p, low):
        size = size_of(d, p)
        return remote(
            o_ref.at[pl.ds(d * ROWS + begins[p][d], size)],
            mixed.at[mine, pl.ds(begins[p][d], size)],
            o_send.at[d, p, low], o_recv.at[mine, p], 4 * group + d, low * 2 + core,
        )

    def local(d, p):
        size = size_of(d, p)
        return pltpu.make_async_copy(
            o_ref.at[pl.ds(d * ROWS + begins[p][d], size)],
            mixed.at[mine, pl.ds(begins[p][d], size)], lsem.at[p],
        )

    def give(tile):
        for d, p in parcels[tile]:
            for low in range(2):
                @pl.when((m != d) | (yl != low))
                def _():
                    out(d, p, low).start()

                @pl.when((m == d) & (yl == low))
                def _():
                    local(d, p).start()

    def landed(g, p, size):
        arrived(mixed.at[g, my_rows(p, size)], o_recv.at[g, p])

    def onward(d, low, p, size):
        g = head(d, low, core)
        ref = mixed.at[g, my_rows(p, size)]
        return remote(ref, ref, pass_send.at[d, p, low], o_recv.at[g, p], seq, mate)

    def sized(p, body):
        if p == 0:
            body(256)
        else:
            @pl.when(outer)
            def _():
                body(size_of(0, p))

            @pl.when((m == 1) | (m == 2))
            def _():
                body(size_of(1, p))

    def relay(p):
        def body(size):
            for d in range(4):
                for low in range(2):
                    @pl.when((m != d) | (yl != low))
                    def _():
                        landed(head(d, low, core), p, size)

                    @pl.when((m == d) & (yl == low))
                    def _():
                        ref = mixed.at[mine, my_rows(p, size)]
                        arrived(ref, lsem.at[p])

                    onward(d, low, p, size).start()

        sized(p, body)

    tiles = GROUP // TILE

    @pl.loop(0, tiles)
    def _(n):
        i = jnp.int32(sequence[-1])
        for k in range(tiles - 1):
            i = jnp.where(n == k, sequence[k], i)
        rows = pl.ds(pl.multiple_of(i * TILE, TILE), TILE)
        first = group * GROUP + i * TILE

        @pl.when(first + TILE <= LONG)
        def _():
            long_tile(i, rows, first)

        @pl.when(first + TILE > LONG)
        def _():
            mixed_tile(i, rows, first)

        for tile in range(tiles):
            @pl.when(i == tile)
            def _():
                give(tile)

        for p in range(2):
            @pl.when(n == jnp.minimum(pick_of(turn_of[p], m) + 2, tiles - 1))
            def _():
                relay(p)

    partner = 1 - core

    def project_out(p):
        def body(size):
            for d in range(4):
                for low in range(2):
                    landed(head(d, low, partner), p, size)
            rows = my_rows(p, size)
            left = jnp.concatenate(
                [mixed[4 * order[k // 4] + k % 4, rows, :] for k in range(16)], axis=1
            )
            y_ref[rows, :] = jnp.dot(
                left, padded[...], preferred_element_type=jnp.float32
            ).astype(jnp.bfloat16)

        sized(p, body)

    project_out(0)
    relay(2)
    project_out(1)
    project_out(2)

    @pl.loop(0, STEPS)
    def _(c):
        to_cross(c).wait_send()
        onward_x(c).wait_send()

    to_mate.wait_send()
    for copy in slabs:
        copy.wait_send()

    @pl.loop(0, 16)
    def _(n):
        c = n // 4
        s = n % 4
        spread(s, c).wait_send()
        spread_q(s, c).wait_send()

        @pl.when(xp == 0)
        def _():
            across(s, c).wait_send()

        @pl.when((xp == 1) & (z > 0))
        def _():
            passed(s, c).wait_send()

        @pl.when((z < 7) & needed(s, c))
        def _():
            ahead(s, c).wait_send()

    @pl.when(xp == 0)
    def _():
        sink_beside.wait_send()

        @pl.when(z < 7)
        def _():
            sink_ahead.wait_send()

    for d in range(4):
        for p in range(3):
            for low in range(2):
                @pl.when((m != d) | (yl != low))
                def _():
                    out(d, p, low).wait_send()

    for p in range(3):
        def body(size):
            for d in range(4):
                for low in range(2):
                    onward(d, low, p, size).wait_send()

        sized(p, body)


def shards(tokens, norm_gain, w_qkv, w_out, sink_logit, segment_ids, positions, padding_mask):
    bf16, f32 = jnp.bfloat16, jnp.float32
    spot = jnp.arange(PAD, dtype=jnp.int32)[None, :]
    info = jnp.where(
        spot == 0, positions[:, None], jnp.where(spot == 1, segment_ids[:, None], padding_mask[:, None])
    ).astype(f32)
    turns = THETA ** (-(np.arange(PAD) % 48) * 2.0 / HD) / (2.0 * np.pi)
    scale = 2.0 ** (np.floor(np.log2(turns)) - 7.0)
    high = np.floor(turns / scale) * scale
    freq = np.zeros((8, PAD), np.float32)
    freq[0] = high
    freq[1] = turns - high

    dma = pltpu.SemaphoreType.DMA
    return pl.pallas_call(
        whole_kernel,
        out_shape=(
            jax.ShapeDtypeStruct((ROWS, PART), bf16),
            jax.ShapeDtypeStruct((2, ROWS, WIDTH), bf16),
        ),
        in_specs=[ANY, VM, ANY, VM, VM, pl.BlockSpec(memory_space=pltpu.SMEM), ANY],
        out_specs=(VM, VM),
        scratch_shapes=[
            pltpu.VMEM((4, ROWS, PART), bf16),
            pltpu.VMEM((4, 3, PART, WIDTH), bf16),
            pltpu.VMEM((ROWS, 3 * WIDTH), f32),
            pltpu.VMEM((ROWS, 1), f32),
            pltpu.VMEM((4, ROWS, PAD), f32),
            pltpu.VMEM((4, ROWS, PAD), bf16),
            pltpu.VMEM((4, ROWS, 2 * PAD), bf16),
            pltpu.VMEM((GROUP, PAD), bf16),
            pltpu.VMEM((SPAN, 2 * PAD), bf16),
            pltpu.VMEM((TILE, WINDOW), f32),
            pltpu.VMEM((GROUP, PAD), bf16),
            pltpu.VMEM((16, ROWS, PAD), bf16),
            pltpu.VMEM((3, WIDTH, PART), bf16),
            pltpu.VMEM((WIDTH, PART), bf16),
            pltpu.VMEM((16 * PAD, PART), bf16),
            dma((5,)), dma, dma((9,)), dma((9,)), dma((3,)), dma((3,)),
            dma((4, 4)), dma((4, 4)), dma((4, 4)), dma((4, 4)),
            dma((4, 4)), dma((4, 4)), dma((4, 4)), dma((4, 4)), dma((2,)), dma,
            dma((4, 3, 2)), dma((16, 3)), dma((4, 3, 2)), dma((3,)),
        ],
        compiler_params=pltpu.CompilerParams(
            collective_id=0, has_side_effects=True, vmem_limit_bytes=62 * 1024 * 1024
        ),
        name="whole",
    )(
        tokens, norm_gain.reshape(1, MODEL), jnp.transpose(w_qkv, (1, 0, 2)), info,
        jnp.asarray(freq), sink_logit, w_out,
    )


def solution(mesh):
    return jax.shard_map(
        shards,
        mesh=mesh,
        in_specs=(
            P("seq", "tp"),
            P(),
            P(None, None, "tp"),
            P("tp", None),
            P("tp"),
            P("seq"),
            P("seq"),
            P("seq"),
        ),
        out_specs=(P("seq", "tp"), P(None, "seq", "tp")),
        check_vma=False,
    )
```

time: 143 us -> 118 us (0.83)
  the two profiles are of different devices: /device:TPU:243 before, /device:TPU:241 now
where the time goes in v3:
time: 118 us; the launch traced here: 117 us
  Pallas kernels  110 us (93%)
  local copies, waits for them, and re-layouts  4.3 us (4%)
  other arithmetic  1.74 us (1%)
    pallas_call x1, Pallas kernels, shards(): pl.pallas_call(whole_kernel, out_shape=(jax.ShapeDtypeStruct((ROWS, PART)...  110 us
    unnamed x2, local copies, waits for them, and re-layouts  4.3 us

profile of v3, /device:TPU:241, one launch (start us, length us, event | category | flops | bytes accessed | tf_op | source)
XLA Modules:
  0.0 116.9 jit_solution(8727100787059190703)
XLA Ops:
  0.6 1.7 %select_convert_fusion.info_ref = f32[576,128]{1,0:T(8,128)} fusion(s32[576]{0:T(1024)} %param.16, s32[576]{0:T(1024)} %param.14, s32[576]{0:T(1024)} %param.15, pred[128]{0:T(512)(128)(4,1)S(1)} %get-tuple-element.2, pred[128]{0:T(512)(128)(4,1)S(1)} %get-tuple-element.3), kind=kLoop, calls=%fused_computation | loop fusion | flops 221184 | bytes 302080 | tf_op jit(solution)/shard_map/convert_element_type | solution.py:694
  2.4 110.2 %whole.1 = (bf16[576,768]{1,0:T(8,128)(2,1)}, bf16[2,576,384]{2,1,0:T(8,128)(2,1)}) custom-call(bf16[576,768]{1,0:T(8,128)(2,1)} %x_ref.1, f32[1,3072]{1,0:T(1,128)} %bitcast.3, bf16[3,3072,384]{2,1,0:T(8,128)(2,1)} %bitcast.2, f32[576,128]{1,0:T(8,128)} %select_convert_fusion.info_ref, f32[8,128]{1,0:T(8,128)} %constant.6.clone.freq_ref, f32[4]{0:T(128)} %logit_ref.1, ...), custom_call_target="tpu_custom_call" | custom-call | tf_op jit(solution)/shard_map/whole/pallas_call | solution.py:703
  112.6 2.1 %copy.13 = bf16[576,768]{1,0:T(8,128)(2,1)} copy(bf16[576,768]{1,0:T(8,128)(2,1)} %get-tuple-element.6) | data formatting | bytes 1769472
  114.7 2.2 %copy.14 = bf16[2,576,384]{2,1,0:T(8,128)(2,1)} copy(bf16[2,576,384]{2,1,0:T(8,128)(2,1)} %get-tuple-element.7) | data formatting | bytes 1769472
  (1 shorter events, 0.0 us)

commit v4 on v3

--- a/solution.py
+++ b/solution.py
@@ -73,10 +73,11 @@
 def whole_kernel(
     x_ref, gain_ref, w_ref, info_ref, freq_ref, logit_ref, wo_ref,
     y_ref, cache_ref,
-    held, weights, acc, square, mark_s, q_s, kv_s, qo, kv, scores, o_ref, mixed, wg, slab, padded,
+    held, weights, acc, square, mark_s, q_s, kv_s, cache_s, qo, kv, scores_a, scores_b, peaks, o_ref, mixed, wg, slab, padded,
     wsem, xsem, send, recv, wsend, wrecv, a_send, a_recv, b_send, b_recv,
-    x_send, z_send, one_recv, two_recv, s_send, s_recv, o_send, o_recv, pass_send, lsem,
+    x_send, z_send, one_recv, two_recv, s_send, s_recv, o_send, o_recv, pass_send, lsem, csem,
 ):
+    scores = (scores_a, scores_b)
     seq, tp, yl, core = place()
     group = seq // 4
     m = seq % 4
@@ -255,8 +256,8 @@
         plain, values = heads(2)
         for n in range(3):
             cols = pl.ds(n * PAD, PAD)
-            cache_ref[0, rows, cols] = (joined[n] * valid).astype(jnp.bfloat16)
-            cache_ref[1, rows, cols] = (plain[n] * valid).astype(jnp.bfloat16)
+            cache_s[0, rows, cols] = joined[n] * valid
+            cache_s[1, rows, cols] = plain[n] * valid
         for h, u in enumerate(values):
             v = jnp.where(lane < HD, u, jnp.where(lane == HD, 1.0, 0.0))
             kv_s[h, rows, PAD:] = v.astype(jnp.bfloat16)
@@ -383,6 +384,9 @@
             @pl.loop(0, 4)
             def _(n):
                 serve((c - 3) * 4 + n)
+
+    cache_copy = pltpu.make_async_copy(cache_s, cache_ref, csem)
+    cache_copy.start()
 
     @pl.loop(8, 20)
     def _(n):
@@ -435,27 +439,43 @@
         out = acc * (1.0 / acc[:, HD:HD + 1])
         o_ref[rows, :] = jnp.where(lane < HD, out, 0.0).astype(jnp.bfloat16)
 
-    def long_tile(i, rows, first):
+    def sink_part(q, first):
+        distance = first + small_down - small_right
+        seen = (small_right < SINKS) & (distance >= WINDOW)
+        return seen, jnp.where(seen, dot_t(q, sink_k), NEG)
+
+    def score(i, slot):
+        rows = pl.ds(pl.multiple_of(i * TILE, TILE), TILE)
+        first = group * GROUP + i * TILE
+        keep = scores[slot]
         q = qo[rows, :]
         near = OWN + i * TILE
         outer = FAR + i * TILE
         s = jnp.where(lower, dot_t(q, key(near, TILE)), dot_t(q, key(outer, TILE)))
-        scores[:, 0:TILE] = s
+        keep[:, 0:TILE] = s
         top = jnp.maximum(s[:, :PAD], s[:, PAD:])
-        distance = first + small_down - small_right
-        seen = (small_right < SINKS) & (distance >= WINDOW)
-        sink_s = jnp.where(seen, dot_t(q, sink_k), NEG)
+        sink_s = sink_part(q, first)[1]
         for c in range(5):
             s = dot_t(q, key(outer + TILE + c * 768, 768))
-            scores[:, pl.ds(TILE + c * 768, 768)] = s
+            keep[:, pl.ds(TILE + c * 768, 768)] = s
             for n in range(6):
                 top = jnp.maximum(top, s[:, n * PAD:(n + 1) * PAD])
-        peak = jnp.maximum(
+        peaks[slot, :, :] = jnp.maximum(
             jnp.max(top, axis=-1, keepdims=True), jnp.max(sink_s, axis=-1, keepdims=True)
         )
+
+    def weigh(i, slot):
+        rows = pl.ds(pl.multiple_of(i * TILE, TILE), TILE)
+        first = group * GROUP + i * TILE
+        keep = scores[slot]
+        q = qo[rows, :]
+        near = OWN + i * TILE
+        outer = FAR + i * TILE
+        peak = peaks[slot, :, :]
+        seen, sink_s = sink_part(q, first)
         w = jnp.where(seen, jnp.exp2(sink_s - peak), 0.0).astype(jnp.bfloat16)
         acc = jnp.dot(w, sink_v, preferred_element_type=jnp.float32)
-        w = jnp.exp2(scores[:, 0:TILE] - peak)
+        w = jnp.exp2(keep[:, 0:TILE] - peak)
         acc += jnp.dot(
             jnp.where(lower, w, 0.0).astype(jnp.bfloat16), val(near, TILE), preferred_element_type=jnp.float32
         )
@@ -463,7 +483,7 @@
             jnp.where(lower, 0.0, w).astype(jnp.bfloat16), val(outer, TILE), preferred_element_type=jnp.float32
         )
         for c in range(5):
-            w = jnp.exp2(scores[:, pl.ds(TILE + c * 768, 768)] - peak).astype(jnp.bfloat16)
+            w = jnp.exp2(keep[:, pl.ds(TILE + c * 768, 768)] - peak).astype(jnp.bfloat16)
             acc += jnp.dot(w, val(outer + TILE + c * 768, 768), preferred_element_type=jnp.float32)
         finish(rows, acc)
 
@@ -480,8 +500,6 @@
         peak = jnp.max(sink_s, axis=-1, keepdims=True)
         w = jnp.where(seen, jnp.exp2(sink_s - peak), 0.0).astype(jnp.bfloat16)
         acc = jnp.dot(w, sink_v, preferred_element_type=jnp.float32)
-        low = jnp.where(first >= LONG, 15, 0)
-
         def step(n, carry):
             peak, acc = carry
             start = FAR + i * TILE + n * TILE
@@ -495,8 +513,11 @@
             acc = acc * jnp.exp2(peak - now) + jnp.dot(w, val(start, TILE), preferred_element_type=jnp.float32)
             return now, acc
 
-        peak, acc = lax.fori_loop(low, 17, step, (peak, acc))
-        finish(rows, acc)
+        peak, acc = lax.fori_loop(15, 17, step, (peak, acc))
+        out = acc * (1.0 / acc[:, HD:HD + 1])
+        out = jnp.where(lane < HD, out, 0.0).astype(jnp.bfloat16)
+        short = first + lax.broadcasted_iota(jnp.int32, (TILE, PAD), 0) >= LONG
+        o_ref[rows, :] = jnp.where(short, out, o_ref[rows, :])
 
     def head(member, low, who):
         b = member // 2
@@ -586,19 +607,40 @@
 
     tiles = GROUP // TILE
 
-    @pl.loop(0, tiles)
-    def _(n):
+    def turn_at(n):
         i = jnp.int32(sequence[-1])
         for k in range(tiles - 1):
             i = jnp.where(n == k, sequence[k], i)
+        return i
+
+    plain = group < 14
+
+    @pl.when(plain)
+    def _():
+        score(jnp.int32(sequence[0]), 0)
+
+    @pl.loop(0, tiles)
+    def _(n):
+        i = turn_at(n)
         rows = pl.ds(pl.multiple_of(i * TILE, TILE), TILE)
         first = group * GROUP + i * TILE
 
-        @pl.when(first + TILE <= LONG)
-        def _():
-            long_tile(i, rows, first)
-
-        @pl.when(first + TILE > LONG)
+        for slot in range(2):
+            @pl.when(plain & (n < tiles - 1) & (n % 2 == slot))
+            def _():
+                score(turn_at(n + 1), 1 - slot)
+                weigh(i, slot)
+
+        @pl.when(plain & (n == tiles - 1))
+        def _():
+            weigh(i, (tiles - 1) % 2)
+
+        @pl.when((group >= 14) & (first < LONG))
+        def _():
+            score(i, 0)
+            weigh(i, 0)
+
+        @pl.when((group >= 14) & (first + TILE > LONG))
         def _():
             mixed_tile(i, rows, first)
 
@@ -623,12 +665,11 @@
             left = jnp.concatenate(
                 [mixed[4 * order[k // 4] + k % 4, rows, :] for k in range(16)], axis=1
             )
-            y_ref[rows, :] = jnp.dot(
-                left, padded[...], preferred_element_type=jnp.float32
-            ).astype(jnp.bfloat16)
+            y_ref[rows, :] = jnp.dot(left, padded[...], preferred_element_type=jnp.float32)
 
         sized(p, body)
 
+    cache_copy.wait()
     project_out(0)
     relay(2)
     project_out(1)
@@ -700,14 +741,14 @@
     freq[1] = turns - high
 
     dma = pltpu.SemaphoreType.DMA
-    return pl.pallas_call(
+    y, cache = pl.pallas_call(
         whole_kernel,
         out_shape=(
-            jax.ShapeDtypeStruct((ROWS, PART), bf16),
-            jax.ShapeDtypeStruct((2, ROWS, WIDTH), bf16),
+            jax.ShapeDtypeStruct((ROWS, PART), f32),
+            jax.ShapeDtypeStruct((2, ROWS, WIDTH), f32),
         ),
         in_specs=[ANY, VM, ANY, VM, VM, pl.BlockSpec(memory_space=pltpu.SMEM), ANY],
-        out_specs=(VM, VM),
+        out_specs=(VM, ANY),
         scratch_shapes=[
             pltpu.VMEM((4, ROWS, PART), bf16),
             pltpu.VMEM((4, 3, PART, WIDTH), bf16),
@@ -716,9 +757,12 @@
             pltpu.VMEM((4, ROWS, PAD), f32),
             pltpu.VMEM((4, ROWS, PAD), bf16),
             pltpu.VMEM((4, ROWS, 2 * PAD), bf16),
+            pltpu.VMEM((2, ROWS, WIDTH), f32),
             pltpu.VMEM((GROUP, PAD), bf16),
             pltpu.VMEM((SPAN, 2 * PAD), bf16),
             pltpu.VMEM((TILE, WINDOW), f32),
+            pltpu.VMEM((TILE, WINDOW), f32),
+            pltpu.VMEM((2, TILE, 1), f32),
             pltpu.VMEM((GROUP, PAD), bf16),
             pltpu.VMEM((16, ROWS, PAD), bf16),
             pltpu.VMEM((3, WIDTH, PART), bf16),
@@ -727,7 +771,7 @@
             dma((5,)), dma, dma((9,)), dma((9,)), dma((3,)), dma((3,)),
             dma((4, 4)), dma((4, 4)), dma((4, 4)), dma((4, 4)),
             dma((4, 4)), dma((4, 4)), dma((4, 4)), dma((4, 4)), dma((2,)), dma,
-            dma((4, 3, 2)), dma((16, 3)), dma((4, 3, 2)), dma((3,)),
+            dma((4, 3, 2)), dma((16, 3)), dma((4, 3, 2)), dma((3,)), dma,
         ],
         compiler_params=pltpu.CompilerParams(
             collective_id=0, has_side_effects=True, vmem_limit_bytes=62 * 1024 * 1024
@@ -737,6 +781,7 @@
         tokens, norm_gain.reshape(1, MODEL), jnp.transpose(w_qkv, (1, 0, 2)), info,
         jnp.asarray(freq), sink_logit, w_out,
     )
+    return (y.astype(bf16), cache.astype(bf16))
 
 
 def solution(mesh):

time: 118 us -> 110 us (0.932)
  Pallas kernels: 110 us -> 103 us
  local copies, waits for them, and re-layouts: 4.3 us -> 0.01 us
  other arithmetic: 1.74 us -> 5.35 us
    pallas_call x1, Pallas kernels: 110 us -> 103 us  [shards(): pl.pallas_call(whole_kernel, out_shape=(jax.ShapeDtypeStruct((ROWS, PART)...]
    unnamed x2, local copies, waits for them, and re-layouts: 4.3 us -> 0.01 us
    convert_element_type x0 -> x2, other arithmetic: none -> 3.61 us  [shards(): return (y.astype(bf16), cache.astype(bf16))]
where the time goes in v4:
time: 110 us; the launch traced here: 109 us
  Pallas kernels  103 us (94%)
  other arithmetic  5.35 us (5%)
    pallas_call x1, Pallas kernels, shards(): pl.pallas_call(whole_kernel, out_shape=(jax.ShapeDtypeStruct((ROWS, PART)...  103 us
    convert_element_type x2, other arithmetic, shards(): return (y.astype(bf16), cache.astype(bf16))  3.61 us

profile of v4, /device:TPU:241, one launch (start us, length us, event | category | flops | bytes accessed | tf_op | source)
XLA Modules:
  0.0 108.7 jit_solution(1877819593271572059)
XLA Ops:
  0.6 1.7 %select_convert_fusion.info_ref = f32[576,128]{1,0:T(8,128)} fusion(s32[576]{0:T(1024)} %param.16, s32[576]{0:T(1024)} %param.14, s32[576]{0:T(1024)} %param.15, pred[128]{0:T(512)(128)(4,1)S(1)} %get-tuple-element.6, pred[128]{0:T(512)(128)(4,1)S(1)} %get-tuple-element.7), kind=kLoop, calls=%fused_computation | loop fusion | flops 221184 | bytes 302080 | tf_op jit(solution)/shard_map/convert_element_type | solution.py:735
  2.4 102.7 %whole.1 = (f32[576,768]{1,0:T(8,128)}, f32[2,576,384]{2,1,0:T(8,128)}) custom-call(bf16[576,768]{1,0:T(8,128)(2,1)} %x_ref.1, f32[1,3072]{1,0:T(1,128)} %bitcast.3, bf16[3,3072,384]{2,1,0:T(8,128)(2,1)} %bitcast.2, f32[576,128]{1,0:T(8,128)} %select_convert_fusion.info_ref, f32[8,128]{1,0:T(8,128)} %constant.6.clone.freq_ref, f32[4]{0:T(128)} %logit_ref.1, ...), custom_call_target="tpu_custom_call" | custom-call | tf_op jit(solution)/shard_map/whole/pallas_call | solution.py:744
  105.1 0.0 copy-start
  105.1 2.6 %convert_element_type.10 = bf16[576,768]{1,0:T(8,128)(2,1)} convert(f32[576,768]{1,0:T(8,128)} %get-tuple-element.4) | non-fusion elementwise | flops 442368 | bytes 2654208 | tf_op jit(solution)/shard_map/convert_element_type | solution.py:784
  107.7 0.0 copy-done
  107.7 1.0 convert_element_type.11
  (1 shorter events, 0.0 us)
Async XLA Ops:
  105.1 2.6 %copy-start = (f32[2,576,384]{2,1,0:T(8,128)S(1)}, f32[2,576,384]{2,1,0:T(8,128)}, u32[]{:S(2)}) copy-start(f32[2,576,384]{2,1,0:T(8,128)} %get-tuple-element.5) | copy-start | bytes 5308420

commit v5 on v4

--- a/solution.py
+++ b/solution.py
@@ -73,9 +73,9 @@
 def whole_kernel(
     x_ref, gain_ref, w_ref, info_ref, freq_ref, logit_ref, wo_ref,
     y_ref, cache_ref,
-    held, weights, acc, square, mark_s, q_s, kv_s, cache_s, qo, kv, scores_a, scores_b, peaks, o_ref, mixed, wg, slab, padded,
+    held, weights, acc, square, mark_s, q_s, kv_s, qo, kv, scores_a, scores_b, peaks, o_ref, mixed, wg, slab, padded,
     wsem, xsem, send, recv, wsend, wrecv, a_send, a_recv, b_send, b_recv,
-    x_send, z_send, one_recv, two_recv, s_send, s_recv, o_send, o_recv, pass_send, lsem, csem,
+    x_send, z_send, one_recv, two_recv, s_send, s_recv, o_send, o_recv, pass_send, lsem,
 ):
     scores = (scores_a, scores_b)
     seq, tp, yl, core = place()
@@ -146,10 +146,8 @@
     to_mate.start()
     slabs = [
         remote(wo_ref.at[:, wide(t2)], wg.at[n], wsend.at[n], wrecv.at[n], s2, t2)
-        for n, (s2, t2) in enumerate(((seq, mate), (flipped, cross), (flipped, far)))
+        for n, (s2, t2) in enumerate(((seq, mate), (seq, cross), (flipped, far)))
     ]
-    for copy in slabs:
-        copy.start()
 
     def blank(start, size):
         mark = lax.broadcasted_iota(jnp.int32, (16, 2 * PAD), 1)
@@ -256,8 +254,8 @@
         plain, values = heads(2)
         for n in range(3):
             cols = pl.ds(n * PAD, PAD)
-            cache_s[0, rows, cols] = joined[n] * valid
-            cache_s[1, rows, cols] = plain[n] * valid
+            cache_ref[0, rows, cols] = joined[n] * valid
+            cache_ref[1, rows, cols] = plain[n] * valid
         for h, u in enumerate(values):
             v = jnp.where(lane < HD, u, jnp.where(lane == HD, 1.0, 0.0))
             kv_s[h, rows, PAD:] = v.astype(jnp.bfloat16)
@@ -376,8 +374,6 @@
             close(c - 1)
             for d in range(4):
                 spread(d, c - 1).start()
-            for d in range(4):
-                spread_q(d, c - 1).start()
 
         @pl.when(c > 2)
         def _():
@@ -385,20 +381,21 @@
             def _(n):
                 serve((c - 3) * 4 + n)
 
-    cache_copy = pltpu.make_async_copy(cache_s, cache_ref, csem)
-    cache_copy.start()
+    @pl.loop(0, STEPS)
+    def _(c):
+        for d in range(4):
+            spread_q(d, c).start()
+
+    for copy in slabs:
+        copy.start()
 
     @pl.loop(8, 20)
     def _(n):
         serve(n)
 
-    for copy in slabs:
-        copy.wait_recv()
     own_slab.wait()
     for n in range(16):
         padded[pl.ds(n * PAD + HD, PAD - HD), :] = jnp.zeros((PAD - HD, PART), jnp.bfloat16)
-    for n in range(12):
-        padded[pl.ds((n + 4) * PAD, HD), :] = wg[n // 4, pl.ds(n % 4 * HD, HD), :]
     for n in range(4):
         padded[pl.ds(n * PAD, HD), :] = slab[pl.ds(n * HD, HD), :]
 
@@ -649,6 +646,13 @@
             def _():
                 give(tile)
 
+        @pl.when(n == tiles - 2)
+        def _():
+            for copy in slabs:
+                copy.wait_recv()
+            for k in range(12):
+                padded[pl.ds((k + 4) * PAD, HD), :] = wg[k // 4, pl.ds(k % 4 * HD, HD), :]
+
         for p in range(2):
             @pl.when(n == jnp.minimum(pick_of(turn_of[p], m) + 2, tiles - 1))
             def _():
@@ -669,7 +673,6 @@
 
         sized(p, body)
 
-    cache_copy.wait()
     project_out(0)
     relay(2)
     project_out(1)
@@ -748,7 +751,7 @@
             jax.ShapeDtypeStruct((2, ROWS, WIDTH), f32),
         ),
         in_specs=[ANY, VM, ANY, VM, VM, pl.BlockSpec(memory_space=pltpu.SMEM), ANY],
-        out_specs=(VM, ANY),
+        out_specs=(VM, VM),
         scratch_shapes=[
             pltpu.VMEM((4, ROWS, PART), bf16),
             pltpu.VMEM((4, 3, PART, WIDTH), bf16),
@@ -757,7 +760,6 @@
             pltpu.VMEM((4, ROWS, PAD), f32),
             pltpu.VMEM((4, ROWS, PAD), bf16),
             pltpu.VMEM((4, ROWS, 2 * PAD), bf16),
-            pltpu.VMEM((2, ROWS, WIDTH), f32),
             pltpu.VMEM((GROUP, PAD), bf16),
             pltpu.VMEM((SPAN, 2 * PAD), bf16),
             pltpu.VMEM((TILE, WINDOW), f32),
@@ -771,7 +773,7 @@
             dma((5,)), dma, dma((9,)), dma((9,)), dma((3,)), dma((3,)),
             dma((4, 4)), dma((4, 4)), dma((4, 4)), dma((4, 4)),
             dma((4, 4)), dma((4, 4)), dma((4, 4)), dma((4, 4)), dma((2,)), dma,
-            dma((4, 3, 2)), dma((16, 3)), dma((4, 3, 2)), dma((3,)), dma,
+            dma((4, 3, 2)), dma((16, 3)), dma((4, 3, 2)), dma((3,)),
         ],
         compiler_params=pltpu.CompilerParams(
             collective_id=0, has_side_effects=True, vmem_limit_bytes=62 * 1024 * 1024

time: 110 us -> 100 us (0.909)
  Pallas kernels: 103 us -> 93 us
    pallas_call x1, Pallas kernels: 103 us -> 93 us  [shards(): pl.pallas_call(whole_kernel, out_shape=(jax.ShapeDtypeStruct((ROWS, PART)...]
where the time goes in v5:
time: 100 us; the launch traced here: 99 us
  Pallas kernels  93 us (93%)
  other arithmetic  5.35 us (5%)
    pallas_call x1, Pallas kernels, shards(): pl.pallas_call(whole_kernel, out_shape=(jax.ShapeDtypeStruct((ROWS, PART)...  93 us
    convert_element_type x2, other arithmetic, shards(): return (y.astype(bf16), cache.astype(bf16))  3.61 us

profile of v5, /device:TPU:241, one launch (start us, length us, event | category | flops | bytes accessed | tf_op | source)
XLA Modules:
  0.0 99.0 jit_solution(5759443741206147636)
XLA Ops:
  0.6 1.7 %select_convert_fusion.info_ref = f32[576,128]{1,0:T(8,128)} fusion(s32[576]{0:T(1024)} %param.16, s32[576]{0:T(1024)} %param.14, s32[576]{0:T(1024)} %param.15, pred[128]{0:T(512)(128)(4,1)S(1)} %get-tuple-element.6, pred[128]{0:T(512)(128)(4,1)S(1)} %get-tuple-element.7), kind=kLoop, calls=%fused_computation | loop fusion | flops 221184 | bytes 302080 | tf_op jit(solution)/shard_map/convert_element_type | solution.py:738
  2.4 93.0 %whole.1 = (f32[576,768]{1,0:T(8,128)}, f32[2,576,384]{2,1,0:T(8,128)}) custom-call(bf16[576,768]{1,0:T(8,128)(2,1)} %x_ref.1, f32[1,3072]{1,0:T(1,128)} %bitcast.3, bf16[3,3072,384]{2,1,0:T(8,128)(2,1)} %bitcast.2, f32[576,128]{1,0:T(8,128)} %select_convert_fusion.info_ref, f32[8,128]{1,0:T(8,128)} %constant.6.clone.freq_ref, f32[4]{0:T(128)} %logit_ref.1, ...), custom_call_target="tpu_custom_call" | custom-call | tf_op jit(solution)/shard_map/whole/pallas_call | solution.py:747
  95.4 0.0 copy-start
  95.4 2.6 %convert_element_type.10 = bf16[576,768]{1,0:T(8,128)(2,1)} convert(f32[576,768]{1,0:T(8,128)} %get-tuple-element.4) | non-fusion elementwise | flops 442368 | bytes 2654208 | tf_op jit(solution)/shard_map/convert_element_type | solution.py:786
  98.0 0.0 copy-done
  98.0 1.0 %convert_element_type.11 = bf16[2,576,384]{2,1,0:T(8,128)(2,1)} convert(f32[2,576,384]{2,1,0:T(8,128)S(1)} %copy-done) | non-fusion elementwise | flops 442368 | bytes 2654208 | tf_op jit(solution)/shard_map/convert_element_type | solution.py:786
  (1 shorter events, 0.0 us)
Async XLA Ops:
  95.4 2.6 %copy-start = (f32[2,576,384]{2,1,0:T(8,128)S(1)}, f32[2,576,384]{2,1,0:T(8,128)}, u32[]{:S(2)}) copy-start(f32[2,576,384]{2,1,0:T(8,128)} %get-tuple-element.5) | copy-start | bytes 5308420
